TPU v7x, 128 devices: a whole 4x4x4 slice. The times are simulated.
128 devices in a mesh: blk: 32 (over x, y, core), grp: 4 (over z).
Axes of the slice: x: 4, y: 4, z: 4, core: 2. Of those that a mesh axis runs over, the one named last changes fastest.
Arguments:
- tensor_blocks: bfloat16 [4608, 64, 4096], P(('blk', 'grp')), may hold values from 0 to 1
- block_coords: int32 [3, 4608], P(None, ('blk', 'grp')), may hold values from 0 to 255, as said below
- block_count: int32 [128], P(('blk', 'grp')), may hold values from 1 to 36, as said below
- row_owner: int32 [3, 256], replicated, may hold values from 0 to 255, as said below
- factors: float32 [3, 16384, 256], P(None, ('blk', 'grp')), may hold values from -2.4 to 2.4
- moment1: float32 [16384, 256], P(('blk', 'grp')), may hold values from -1.8 to 1.8
- moment2: float32 [16384, 256], P(('blk', 'grp')), may hold values from 0.01 to 1
Outputs:
- new_factor: float32 [16384, 256], P(('blk', 'grp'))
- new_moment1: float32 [16384, 256], P(('blk', 'grp'))
- new_moment2: float32 [16384, 256], P(('blk', 'grp'))
Inputs may be any that keep to these rules, and one draw needn't show every extreme that they name: `row_owner`: for each mode a permutation; storage position p lies on device p // 2 of blk+grp. `block_coords`: of the 108 row blocks named by one device's slots, at most 2 have positions on any one device, and exactly 2 on some device; of the 36 first-mode row blocks named by one device's slots, at most 1 have positions on any one device, and exactly 1 on some device. `block_count`: some device has all slots live.
All inputs are finite; a program needn't handle non-finite values.
Results may differ from a plain program's by a relative error of at most 0.0012.
Values may be sent and summed in bfloat16 or wider, within the bound.
A program may use at most 128 MiB of HBM per device.

v0:
```python
import jax
import jax.numpy as jnp
from jax import lax
from jax.sharding import PartitionSpec as P


def route_requests(values):
    return lax.all_to_all(values, ("blk", "grp"), split_axis=0, concat_axis=0, tiled=True)


def route_rows(values):
    return lax.all_to_all(values, ("blk", "grp"), split_axis=0, concat_axis=0, tiled=True)


def route_partials(values):
    return lax.all_to_all(values, ("blk", "grp"), split_axis=0, concat_axis=0, tiled=True)


def group_width(slot_count):
    best = 1
    for width in range(1, 9):
        if slot_count % width == 0:
            best = width
    return best


def per_device(tensor_blocks, block_coords, block_count, row_owner, factors, moment1, moment2):
    slot_count = tensor_blocks.shape[0]
    edge = tensor_blocks.shape[1]
    rank = factors.shape[2]
    devices = lax.axis_size(("blk", "grp"))
    local_blocks = moment1.shape[0] // edge
    capacity = (3 * slot_count + devices - 1) // devices + 1
    first_cap = (slot_count + devices - 1) // devices
    buffer_len = devices * capacity
    first_len = devices * first_cap
    wanted = 3 * slot_count
    positions = jnp.concatenate([jnp.take(row_owner[m], block_coords[m]) for m in range(3)])
    owners = positions // local_blocks
    local_index = positions % local_blocks + jnp.repeat(
        jnp.arange(3, dtype=jnp.int32) * local_blocks, slot_count
    )
    order = jnp.arange(wanted, dtype=jnp.int32)
    earlier = order[None, :] < order[:, None]
    standing = jnp.sum(((owners[None, :] == owners[:, None]) & earlier).astype(jnp.int32), axis=1)
    buffer_index = owners * capacity + standing
    requests = jnp.full((buffer_len,), -1, jnp.int32).at[buffer_index].set(local_index)
    incoming = route_requests(requests)
    table = factors.reshape(3 * local_blocks, edge, rank).astype(jnp.bfloat16)
    present = incoming >= 0
    reply = jnp.where(
        present[:, None, None],
        jnp.take(table, jnp.maximum(incoming, 0), axis=0),
        jnp.zeros((), jnp.bfloat16),
    )
    fetched = route_rows(reply)
    gathered = jnp.take(fetched, buffer_index, axis=0).reshape(3, slot_count, edge, rank)
    alive = (jnp.arange(slot_count, dtype=jnp.int32) < block_count[0]).astype(jnp.float32)
    width = group_width(slot_count)
    groups = slot_count // width
    grouped_blocks = tensor_blocks.reshape(groups, width, edge, edge * edge)
    grouped_rows = gathered.reshape(3, groups, width, edge, rank)
    grouped_alive = alive.reshape(groups, width)

    def group_step(carry, item):
        block, rows_a, rows_b, rows_c, weight = item
        pair = (
            (rows_b.astype(jnp.float32)[:, :, None, :] * rows_c.astype(jnp.float32)[:, None, :, :])
            .reshape(width, edge * edge, rank)
            .astype(jnp.bfloat16)
        )
        model = lax.dot_general(
            rows_a, pair, (((2,), (2,)), ((0,), (0,))), preferred_element_type=jnp.float32
        )
        resid = (
            (jax.nn.sigmoid(model) - block.astype(jnp.float32)) * weight[:, None, None]
        ).astype(jnp.bfloat16)
        return (
            carry,
            lax.dot_general(
                resid, pair, (((2,), (1,)), ((0,), (0,))), preferred_element_type=jnp.float32
            ),
        )

    _, parts = lax.scan(
        group_step,
        0.0,
        (grouped_blocks, grouped_rows[0], grouped_rows[1], grouped_rows[2], grouped_alive),
    )
    parts = parts.reshape(slot_count, edge, rank)
    first_index = owners[:slot_count] * first_cap + standing[:slot_count]
    outgoing = jnp.zeros((first_len, edge, rank), jnp.float32).at[first_index].set(parts)
    arrived = route_partials(outgoing)
    first_requests = incoming.reshape(devices, capacity)[:, :first_cap].reshape(first_len)
    targets = jnp.arange(local_blocks, dtype=jnp.int32)
    select = (first_requests[None, :] == targets[:, None]).astype(jnp.float32)
    grad = jnp.dot(select, arrived.reshape(first_len, edge * rank), precision=lax.Precision.HIGHEST)
    grad = grad.reshape(local_blocks * edge, rank)
    new_moment1 = 0.9 * moment1 + 0.1 * grad
    new_moment2 = 0.999 * moment2 + 0.001 * grad * grad
    new_factor = factors[0] - 0.02 * (new_moment1 / (1.0 - 0.9**8)) / (
        jnp.sqrt(new_moment2 / (1.0 - 0.999**8)) + 1e-08
    )
    return (new_factor, new_moment1, new_moment2)


def solution(mesh):
    return jax.shard_map(
        per_device,
        mesh=mesh,
        in_specs=(
            P(("blk", "grp"), None, None),
            P(None, ("blk", "grp")),
            P(("blk", "grp")),
            P(),
            P(None, ("blk", "grp"), None),
            P(("blk", "grp"), None),
            P(("blk", "grp"), None),
        ),
        out_specs=(P(("blk", "grp"), None), P(("blk", "grp"), None), P(("blk", "grp"), None)),
        check_vma=False,
    )
```

profile of v0, /device:TPU:0, one launch (start us, length us, event | category | flops | bytes accessed | tf_op | source)
XLA Modules:
  0.0 445.0 jit_solution(12329375492152040212)
XLA Ops:
  1.6 0.8 fusion.23
  4.8 0.8 and_select_fusion.2
  6.0 0.9 scatter_custom_fusion
  7.7 11.1 %all-to-all-start = ((s32[128,2,1]{1,2,0:T(1,128)}), s32[128,2,1]{1,2,0:T(1,128)S(1)}, u32[]{:S(2)}, u32[]{:S(2)}) async-start(s32[128,2,1]{1,2,0:T(1,128)} %bitcast.19), calls=%async_computation | async-start | bytes 131072 | tf_op jit(solution)/shard_map/all_to_all | solution.py:8
  18.8 1.0 convert_element_type.50
  19.8 8.0 %all-to-all-done = s32[128,2,1]{1,2,0:T(1,128)S(1)} async-done(((s32[128,2,1]{1,2,0:T(1,128)}), s32[128,2,1]{1,2,0:T(1,128)S(1)}, u32[]{:S(2)}, u32[]{:S(2)}) %all-to-all-start) | async-done | bytes 1056 | tf_op jit(solution)/shard_map/all_to_all | solution.py:8
  28.9 8.4 %gather_fusion = bf16[256,64,256]{2,1,0:T(8,128)(2,1)} fusion(bf16[6,64,256]{2,1,0:T(8,128)(2,1)S(1)} %bitcast.82, s32[1024]{0:T(1024)S(1)} %pad_clamp_fusion.1), kind=kCustom, calls=%fused_computation.3 | custom fusion | bytes 16778240 | tf_op jit(solution)/shard_map/jit(_take)/gather | solution.py:53
  37.3 7.6 %select_select_fusion = bf16[256,64,256]{2,1,0:T(8,128)(2,1)} fusion(bf16[256,64,256]{2,1,0:T(8,128)(2,1)} %gather_fusion, pred[256]{0:T(512)(128)(4,1)S(1)} %le.36, pred[256]{0:T(512)(128)(4,1)S(1)} %ge.33), kind=kLoop, calls=%fused_computation.21 | loop fusion | flops 8388608 | bytes 16777728 | tf_op jit(solution)/shard_map/jit(_where)/select_n | solution.py:51
  44.9 6.1 %all-to-all-start.1 = ((bf16[256,64,256]{2,1,0:T(8,128)(2,1)}), bf16[256,64,256]{2,1,0:T(8,128)(2,1)}, u32[]{:S(2)}, u32[]{:S(2)}) async-start(bf16[256,64,256]{2,1,0:T(8,128)(2,1)} %select_select_fusion), calls=%async_computation.1 | async-start | bytes 16777216 | tf_op jit(solution)/shard_map/all_to_all | solution.py:12
  51.8 106.2 %all-to-all-done.1 = bf16[256,64,256]{2,1,0:T(8,128)(2,1)} async-done(((bf16[256,64,256]{2,1,0:T(8,128)(2,1)}), bf16[256,64,256]{2,1,0:T(8,128)(2,1)}, u32[]{:S(2)}, u32[]{:S(2)}) %all-to-all-start.1) | async-done | bytes 8388640 | tf_op jit(solution)/shard_map/all_to_all | solution.py:12
  158.0 4.2 gather_fusion.1
  162.6 1.4 fusion.22
  164.0 140.0 %while.10 = (s32[]{:T(128)}, f32[6,6,64,256]{3,2,1,0:T(8,128)}, bf16[6,6,64,256]{3,2,1,0:T(8,128)(2,1)}, bf16[6,6,64,256]{3,2,1,0:T(8,128)(2,1)S(1)}, bf16[6,6,6...) while((s32[]{:T(128)}, f32[6,6,64,256]{3,2,1,0:T(8,128)}, ...), condition=%wide.region_3.5_spmd, body=%wide.region_2.4_spmd.sunk | while | flops 1634402304 | bytes 43452076 | solution.py:85
  164.1 10.3 %multiply_convert_fusion.2 = bf16[6,64,64,256]{3,2,1,0:T(8,128)(2,1)} fusion(f32[6,64,256]{2,1,0:T(8,128)S(1)} %get-tuple-element.124, f32[6,64,256]{2,1,0:T(8,128)S(1)} %get-tuple-element.125), kind=kLoop, calls=%fused_computation.7.clone.1 | loop fusion | flops 12582912 | bytes 13369344 | tf_op jit(solution)/shard_map/while/body/eval_jaxpr/convert_element_type | solution.py:70
  174.3 13.0 %fusion.36 = f32[6,6,64,256]{3,2,1,0:T(8,128)} fusion(f32[6,6,64,256]{3,2,1,0:T(8,128)} %get-tuple-element.135, s32[]{:T(128)S(6)} %copy.16, bf16[6,4096,256]{2,1,0:T(8,128)(2,1)} %bitcast.83, f32[6]{0:T(128)S(1)} %fusion.35, bf16[6,6,64,4096]{3,2,1,0:T(8,128)(2,1)} %get-tuple-element.147, bf16[6,6,64,256]{3,2,1,0:T(8,128)(2,1)} %get-tuple-element.144), kind=kOutput, calls=%fused_computation.12.clone.1 | convolution fusion | flops 1621622784 | bytes 28902936 | tf_op jit(solution)/shard_map/while/body/eval_jaxpr/dot_general | solution.py:80
  187.4 10.3 %multiply_convert_fusion.2 = bf16[6,64,64,256]{3,2,1,0:T(8,128)(2,1)} fusion(f32[6,64,256]{2,1,0:T(8,128)S(1)} %get-tuple-element.124, f32[6,64,256]{2,1,0:T(8,128)S(1)} %get-tuple-element.125), kind=kLoop, calls=%fused_computation.7.clone.1 | loop fusion | flops 12582912 | bytes 13369344 | tf_op jit(solution)/shard_map/while/body/eval_jaxpr/convert_element_type | solution.py:70
  197.7 13.0 %fusion.36 = f32[6,6,64,256]{3,2,1,0:T(8,128)} fusion(f32[6,6,64,256]{3,2,1,0:T(8,128)} %get-tuple-element.135, s32[]{:T(128)S(6)} %copy.16, bf16[6,4096,256]{2,1,0:T(8,128)(2,1)} %bitcast.83, f32[6]{0:T(128)S(1)} %fusion.35, bf16[6,6,64,4096]{3,2,1,0:T(8,128)(2,1)} %get-tuple-element.147, bf16[6,6,64,256]{3,2,1,0:T(8,128)(2,1)} %get-tuple-element.144), kind=kOutput, calls=%fused_computation.12.clone.1 | convolution fusion | flops 1621622784 | bytes 28902936 | tf_op jit(solution)/shard_map/while/body/eval_jaxpr/dot_general | solution.py:80
  210.7 10.3 %multiply_convert_fusion.2 = bf16[6,64,64,256]{3,2,1,0:T(8,128)(2,1)} fusion(f32[6,64,256]{2,1,0:T(8,128)S(1)} %get-tuple-element.124, f32[6,64,256]{2,1,0:T(8,128)S(1)} %get-tuple-element.125), kind=kLoop, calls=%fused_computation.7.clone.1 | loop fusion | flops 12582912 | bytes 13369344 | tf_op jit(solution)/shard_map/while/body/eval_jaxpr/convert_element_type | solution.py:70
  221.0 12.9 %fusion.36 = f32[6,6,64,256]{3,2,1,0:T(8,128)} fusion(f32[6,6,64,256]{3,2,1,0:T(8,128)} %get-tuple-element.135, s32[]{:T(128)S(6)} %copy.16, bf16[6,4096,256]{2,1,0:T(8,128)(2,1)} %bitcast.83, f32[6]{0:T(128)S(1)} %fusion.35, bf16[6,6,64,4096]{3,2,1,0:T(8,128)(2,1)} %get-tuple-element.147, bf16[6,6,64,256]{3,2,1,0:T(8,128)(2,1)} %get-tuple-element.144), kind=kOutput, calls=%fused_computation.12.clone.1 | convolution fusion | flops 1621622784 | bytes 28902936 | tf_op jit(solution)/shard_map/while/body/eval_jaxpr/dot_general | solution.py:80
  234.0 10.3 %multiply_convert_fusion.2 = bf16[6,64,64,256]{3,2,1,0:T(8,128)(2,1)} fusion(f32[6,64,256]{2,1,0:T(8,128)S(1)} %get-tuple-element.124, f32[6,64,256]{2,1,0:T(8,128)S(1)} %get-tuple-element.125), kind=kLoop, calls=%fused_computation.7.clone.1 | loop fusion | flops 12582912 | bytes 13369344 | tf_op jit(solution)/shard_map/while/body/eval_jaxpr/convert_element_type | solution.py:70
  244.3 13.0 %fusion.36 = f32[6,6,64,256]{3,2,1,0:T(8,128)} fusion(f32[6,6,64,256]{3,2,1,0:T(8,128)} %get-tuple-element.135, s32[]{:T(128)S(6)} %copy.16, bf16[6,4096,256]{2,1,0:T(8,128)(2,1)} %bitcast.83, f32[6]{0:T(128)S(1)} %fusion.35, bf16[6,6,64,4096]{3,2,1,0:T(8,128)(2,1)} %get-tuple-element.147, bf16[6,6,64,256]{3,2,1,0:T(8,128)(2,1)} %get-tuple-element.144), kind=kOutput, calls=%fused_computation.12.clone.1 | convolution fusion | flops 1621622784 | bytes 28902936 | tf_op jit(solution)/shard_map/while/body/eval_jaxpr/dot_general | solution.py:80
  257.4 10.3 %multiply_convert_fusion.2 = bf16[6,64,64,256]{3,2,1,0:T(8,128)(2,1)} fusion(f32[6,64,256]{2,1,0:T(8,128)S(1)} %get-tuple-element.124, f32[6,64,256]{2,1,0:T(8,128)S(1)} %get-tuple-element.125), kind=kLoop, calls=%fused_computation.7.clone.1 | loop fusion | flops 12582912 | bytes 13369344 | tf_op jit(solution)/shard_map/while/body/eval_jaxpr/convert_element_type | solution.py:70
  267.6 13.0 %fusion.36 = f32[6,6,64,256]{3,2,1,0:T(8,128)} fusion(f32[6,6,64,256]{3,2,1,0:T(8,128)} %get-tuple-element.135, s32[]{:T(128)S(6)} %copy.16, bf16[6,4096,256]{2,1,0:T(8,128)(2,1)} %bitcast.83, f32[6]{0:T(128)S(1)} %fusion.35, bf16[6,6,64,4096]{3,2,1,0:T(8,128)(2,1)} %get-tuple-element.147, bf16[6,6,64,256]{3,2,1,0:T(8,128)(2,1)} %get-tuple-element.144), kind=kOutput, calls=%fused_computation.12.clone.1 | convolution fusion | flops 1621622784 | bytes 28902936 | tf_op jit(solution)/shard_map/while/body/eval_jaxpr/dot_general | solution.py:80
  280.7 10.3 %multiply_convert_fusion.2 = bf16[6,64,64,256]{3,2,1,0:T(8,128)(2,1)} fusion(f32[6,64,256]{2,1,0:T(8,128)S(1)} %get-tuple-element.124, f32[6,64,256]{2,1,0:T(8,128)S(1)} %get-tuple-element.125), kind=kLoop, calls=%fused_computation.7.clone.1 | loop fusion | flops 12582912 | bytes 13369344 | tf_op jit(solution)/shard_map/while/body/eval_jaxpr/convert_element_type | solution.py:70
  291.0 13.0 %fusion.36 = f32[6,6,64,256]{3,2,1,0:T(8,128)} fusion(f32[6,6,64,256]{3,2,1,0:T(8,128)} %get-tuple-element.135, s32[]{:T(128)S(6)} %copy.16, bf16[6,4096,256]{2,1,0:T(8,128)(2,1)} %bitcast.83, f32[6]{0:T(128)S(1)} %fusion.35, bf16[6,6,64,4096]{3,2,1,0:T(8,128)(2,1)} %get-tuple-element.147, bf16[6,6,64,256]{3,2,1,0:T(8,128)(2,1)} %get-tuple-element.144), kind=kOutput, calls=%fused_computation.12.clone.1 | convolution fusion | flops 1621622784 | bytes 28902936 | tf_op jit(solution)/shard_map/while/body/eval_jaxpr/dot_general | solution.py:80
  304.0 4.3 broadcast_in_dim.69
  308.3 7.6 %scatter_fusion = f32[128,64,256]{2,1,0:T(8,128)} fusion(f32[128,64,256]{2,1,0:T(8,128)} %broadcast_in_dim.69, s32[36]{0:T(128)S(1)} %compare_select_fusion.4, f32[36,64,256]{2,1,0:T(8,128)S(1)} %bitcast.90), kind=kCustom, calls=%fused_computation.6 | custom fusion | bytes 7078032 | tf_op jit(solution)/shard_map/scatter | solution.py:92
  315.9 7.7 %all-to-all-start.2 = ((f32[128,64,256]{2,1,0:T(8,128)}), f32[128,64,256]{2,1,0:T(8,128)}, u32[]{:S(2)}, u32[]{:S(2)}) async-start(f32[128,64,256]{2,1,0:T(8,128)} %scatter_fusion), calls=%async_computation.2 | async-start | bytes 16777216 | tf_op jit(solution)/shard_map/all_to_all | solution.py:16
  323.7 106.7 %all-to-all-done.2 = f32[128,64,256]{2,1,0:T(8,128)} async-done(((f32[128,64,256]{2,1,0:T(8,128)}), f32[128,64,256]{2,1,0:T(8,128)}, u32[]{:S(2)}, u32[]{:S(2)}) %all-to-all-start.2) | async-done | bytes 8388640 | tf_op jit(solution)/shard_map/all_to_all | solution.py:16
  430.5 9.9 %copy.12 = f32[16,8,64,256]{3,1,2,0:T(8,128)S(1)} copy(f32[16,8,64,256]{3,2,1,0:T(8,128)} %bitcast.31) | data formatting | bytes 16777216
  440.4 2.8 fusion.13
  443.3 1.7 bitcast_subtract_fusion
  (50 shorter events, 6.7 us)
Async XLA Ops:
  7.7 20.1 %all-to-all-start = ((s32[128,2,1]{1,2,0:T(1,128)}), s32[128,2,1]{1,2,0:T(1,128)S(1)}, u32[]{:S(2)}, u32[]{:S(2)}) async-start(s32[128,2,1]{1,2,0:T(1,128)} %bitcast.19), calls=%async_computation | async-start | bytes 131072 | tf_op jit(solution)/shard_map/all_to_all | solution.py:8
  27.8 9.5 %copy-start.1 = (s32[128,2,1]{1,2,0:T(1,128)}, s32[128,2,1]{1,2,0:T(1,128)S(1)}, u32[]{:S(2)}) copy-start(s32[128,2,1]{1,2,0:T(1,128)S(1)} %all-to-all-done) | copy-start | bytes 3076
  44.9 113.0 %all-to-all-start.1 = ((bf16[256,64,256]{2,1,0:T(8,128)(2,1)}), bf16[256,64,256]{2,1,0:T(8,128)(2,1)}, u32[]{:S(2)}, u32[]{:S(2)}) async-start(bf16[256,64,256]{2,1,0:T(8,128)(2,1)} %select_select_fusion), calls=%async_computation.1 | async-start | bytes 16777216 | tf_op jit(solution)/shard_map/all_to_all | solution.py:12
  304.0 4.3 copy-start
  315.9 7.7 %copy-start.2 = (s32[128,2,1]{1,2,0:T(1,128)S(1)}, s32[128,2,1]{1,2,0:T(1,128)}, u32[]{:S(2)}) copy-start(s32[128,2,1]{1,2,0:T(1,128)} %copy-done.1) | copy-start | bytes 3076
  315.9 114.6 %all-to-all-start.2 = ((f32[128,64,256]{2,1,0:T(8,128)}), f32[128,64,256]{2,1,0:T(8,128)}, u32[]{:S(2)}, u32[]{:S(2)}) async-start(f32[128,64,256]{2,1,0:T(8,128)} %scatter_fusion), calls=%async_computation.2 | async-start | bytes 16777216 | tf_op jit(solution)/shard_map/all_to_all | solution.py:16
  440.3 3.0 copy-start.3
  440.3 3.0 copy-start.4
where the time goes:
time: 446 us; the launch traced here: 445 us
  waiting for transfers between devices  221 us (50%)
  matrix products  80.7 us (18%)
  other arithmetic  75.5 us (17%)
  local copies, waits for them, and re-layouts  41.5 us (9%)
  starting transfers between devices  24.9 us (6%)
    all_to_all x1, waiting for transfers between devices, route_partials(): lax.all_to_all(values, ('blk', 'grp'), split_axis=0, concat_axis=0, tiled...  107 us
    all_to_all x1, waiting for transfers between devices, route_rows(): lax.all_to_all(values, ('blk', 'grp'), split_axis=0, concat_axis=0, tiled...  106 us
    dot_general x6, matrix products, group_step(): lax.dot_general(resid, pair, (((2,), (1,)), ((0,), (0,))), preferred_elem...  77.9 us
    convert_element_type x6, other arithmetic, group_step(): pair = (rows_b.astype(jnp.float32)[:, :, None, :] * rows_c.astype(jnp.flo...  61.7 us
    all_to_all x1, starting transfers between devices, route_requests(): lax.all_to_all(values, ('blk', 'grp'), split_axis=0, concat_axis=0, tiled...  11.1 us
    unnamed x11, local copies, waits for them, and re-layouts  9.89 us
  transfers between devices with their start and end apart: 3, of which 3 were waited for; matrix products, arithmetic and copies ran while one was open for 0% of the time, Pallas kernels for 0%

commit v1 on v0

v1 whole, which is shorter than its diff:
```python
import functools

import jax
import jax.numpy as jnp
from jax import lax
from jax.experimental import pallas as pl
from jax.experimental.pallas import tpu as pltpu
from jax.sharding import PartitionSpec as P

AXES = ("blk", "grp")


def block_kernel(edge, chunk, where_ref, count_ref, block_ref, a_ref, b_ref, c_ref, zero_ref, out_ref):
    slot = pl.program_id(0)

    @pl.when(slot < count_ref[0])
    def _():
        half_a = a_ref[0] * jnp.bfloat16(0.5)
        rows_c = c_ref[0]
        rank = rows_c.shape[1]
        total = jnp.zeros((edge, rank), jnp.float32)
        for step in range(edge // chunk):
            pair = jnp.concatenate(
                [b_ref[0, pl.ds(step * chunk + j, 1), :] * rows_c for j in range(chunk)], axis=0
            )
            model = lax.dot_general(
                half_a, pair, (((1,), (1,)), ((), ())), preferred_element_type=jnp.float32
            )
            width = chunk * edge
            observed = block_ref[0, :, step * width : (step + 1) * width].astype(jnp.float32)
            resid = (0.5 * jnp.tanh(model) + (0.5 - observed)).astype(jnp.bfloat16)
            total = total + jnp.dot(resid, pair, preferred_element_type=jnp.float32)
        out_ref[0] = total

    @pl.when(slot >= count_ref[0])
    def _():
        out_ref[...] = jnp.zeros_like(out_ref)


def block_gradients(tensor_blocks, table, where, count, zeros):
    slots, edge, merged = tensor_blocks.shape
    rank = table.shape[2]
    spec = lambda m: pl.BlockSpec((1, edge, rank), lambda s, w, n: (w[m, s], 0, 0))
    return pl.pallas_call(
        functools.partial(block_kernel, edge, 8),
        out_shape=jax.ShapeDtypeStruct(zeros.shape, jnp.float32),
        grid_spec=pltpu.PrefetchScalarGridSpec(
            num_scalar_prefetch=2,
            grid=(slots,),
            in_specs=[
                pl.BlockSpec((1, edge, merged), lambda s, w, n: (s, 0, 0)),
                spec(0),
                spec(1),
                spec(2),
                pl.BlockSpec(memory_space=pl.ANY),
            ],
            out_specs=pl.BlockSpec((1, edge, rank), lambda s, w, n: (w[3, s], 0, 0)),
        ),
        input_output_aliases={6: 0},
        compiler_params=pltpu.CompilerParams(
            dimension_semantics=("arbitrary",), vmem_limit_bytes=48 << 20
        ),
        cost_estimate=pl.CostEstimate(
            flops=4 * slots * edge * merged * rank,
            bytes_accessed=2 * slots * edge * (merged + 5 * rank),
            transcendentals=slots * edge * merged,
        ),
    )(where, count, tensor_blocks, table, table, table, zeros)


def per_device(tensor_blocks, block_coords, block_count, row_owner, factors, moment1, moment2):
    slot_count, edge, _ = tensor_blocks.shape
    modes, _, rank = factors.shape
    devices = lax.axis_size(AXES)
    local_blocks = moment1.shape[0] // edge
    blocks = devices * local_blocks
    pos = jnp.take_along_axis(row_owner, block_coords, axis=1)
    mode = jnp.arange(modes, dtype=jnp.int32)[:, None]
    where = (pos // local_blocks) * (modes * local_blocks) + mode * local_blocks + pos % local_blocks
    where = jnp.concatenate([where, pos[:1]], axis=0)
    table = lax.all_gather(factors.astype(jnp.bfloat16), AXES, axis=0, tiled=False)
    table = table.reshape(modes * blocks, edge, rank)
    zeros = jnp.zeros((blocks, edge, rank), jnp.float32)
    parts = block_gradients(tensor_blocks, table, where, block_count, zeros)
    grad = lax.psum_scatter(
        parts.reshape(blocks * edge, rank), AXES, scatter_dimension=0, tiled=True
    )
    new_moment1 = 0.9 * moment1 + 0.1 * grad
    new_moment2 = 0.999 * moment2 + 0.001 * grad * grad
    new_factor = factors[0] - 0.02 * (new_moment1 / (1.0 - 0.9**8)) / (
        jnp.sqrt(new_moment2 / (1.0 - 0.999**8)) + 1e-08
    )
    return (new_factor, new_moment1, new_moment2)


def solution(mesh):
    return jax.shard_map(
        per_device,
        mesh=mesh,
        in_specs=(
            P(AXES, None, None),
            P(None, AXES),
            P(AXES),
            P(),
            P(None, AXES, None),
            P(AXES, None),
            P(AXES, None),
        ),
        out_specs=(P(AXES, None), P(AXES, None), P(AXES, None)),
        check_vma=False,
    )
```

time: 446 us -> 846 us (1.90)
  waiting for transfers between devices: 221 us -> 767 us
  matrix products: 80.7 us -> 0 us
  other arithmetic: 75.5 us -> 4.93 us
  Pallas kernels: 0 us -> 49.1 us
  local copies, waits for them, and re-layouts: 41.5 us -> 10.1 us
  starting transfers between devices: 24.9 us -> 0.08 us
  between operations: 1.48 us -> 14.7 us
    reduce_scatter x0 -> x1, waiting for transfers between devices: none -> 673 us  [per_device(): lax.psum_scatter(parts.reshape(blocks * edge, rank), AXES, scatter_dimens...]
    all_to_all x3 -> x0, waiting for transfers between devices: 221 us -> none  [the longest x1 107 us: route_partials(): lax.all_to_all(values, ('blk', 'grp'), split_axis=0, concat_axis=0, tiled...]
    all_gather x0 -> x1, waiting for transfers between devices: none -> 93.3 us  [per_device(): lax.all_gather(factors.astype(jnp.bfloat16), AXES, axis=0, tiled=False)]
    dot_general x7 -> x0, matrix products: 80.7 us -> none  [the longest x6 77.9 us: group_step(): lax.dot_general(resid, pair, (((2,), (1,)), ((0,), (0,))), preferred_elem...]
    convert_element_type x14 -> x1, other arithmetic: 63.1 us -> 1.71 us  [per_device(): factors.astype(jnp.bfloat16)]
    pallas_call x0 -> x1, Pallas kernels: none -> 49.1 us  [block_gradients(): pl.pallas_call(functools.partial(block_kernel, edge, 8), out_shape=jax.Sh...]
    all_to_all x3 -> x0, starting transfers between devices: 24.9 us -> none  [the longest x1 11.1 us: route_requests(): lax.all_to_all(values, ('blk', 'grp'), split_axis=0, concat_axis=0, tiled...]
    gather x5 -> x3, local copies, waits for them, and re-layouts: 15 us -> 2.2 us  [per_device(): pos = jnp.take_along_axis(row_owner, block_coords, axis=1)]
  transfers between devices with their start and end apart: 3 -> 2, of which waited for: 3 -> 2; matrix products, arithmetic and copies ran while one was open for 0% -> 0% of each run, Pallas kernels for 0% -> 0%
where the time goes in v1:
time: 846 us; the launch traced here: 845 us
  waiting for transfers between devices  767 us (91%)
  Pallas kernels  49.1 us (6%)
  between operations  14.7 us (2%)
  local copies, waits for them, and re-layouts  10.1 us (1%)
    reduce_scatter x1, waiting for transfers between devices, per_device(): lax.psum_scatter(parts.reshape(blocks * edge, rank), AXES, scatter_dimens...  673 us
    all_gather x1, waiting for transfers between devices, per_device(): lax.all_gather(factors.astype(jnp.bfloat16), AXES, axis=0, tiled=False)  93.3 us
    pallas_call x1, Pallas kernels, block_gradients(): pl.pallas_call(functools.partial(block_kernel, edge, 8), out_shape=jax.Sh...  49.1 us
  transfers between devices with their start and end apart: 2, of which 2 were waited for; matrix products, arithmetic and copies ran while one was open for 0% of the time, Pallas kernels for 0%

profile of v1, /device:TPU:0, one launch (start us, length us, event | category | flops | bytes accessed | tf_op | source)
XLA Modules:
  0.0 845.4 jit_solution(10306358621258942504)
XLA Ops:
  7.2 0.0 copy-start
  7.2 0.0 all-gather.3.cloned.1.call-start
  7.2 1.7 convert_element_type.3
  8.9 0.0 all-gather.3.cloned.1.call-update
  9.0 0.0 reduce-scatter.2.cloned.1.call-start
  9.7 0.7 bitcast_or_fusion
  10.3 0.1 reshape.29
  10.4 0.0 copy-done
  10.4 2.0 gather_fusion
  12.5 0.1 reshape.32
  12.6 0.8 fusion.3
  13.3 93.3 %all-gather.3.cloned.1.call-done = bf16[384,128,256]{2,1,0:T(8,128)(2,1)} async-done(((bf16[3,128,256]{2,1,0:T(8,128)(2,1)}), bf16[384,128,256]{2,1,0:T(8,128)(2,1)}) %all-gather.3.cloned.1.call-update) | async-done | bytes 25165840 | tf_op jit(solution)/shard_map/all_gather | solution.py:81
  106.7 7.8 broadcast_in_dim.9.zero_ref
  114.5 0.0 copy-start.1
  114.5 0.0 copy-start.2
  114.5 49.1 %shard_map.94 = f32[256,64,256]{2,1,0:T(8,128)} custom-call(s32[4,36]{1,0:T(4,128)S(1)} %pad_add_fusion.where_ref, s32[1]{0:T(128)S(6)} %copy.12.count_ref, bf16[36,64,4096]{2,1,0:T(8,128)(2,1)} %block_ref.1, bf16[768,64,256]{2,1,0:T(8,128)(2,1)} %bitcast.8, bf16[768,64,256]{2,1,0:T(8,128)(2,1)} %bitcast.9, ...), custom_call_target="tpu_custom_call", output_to_operand_aliasing={{}: (6, {})} | custom-call | flops 9663676416 | bytes 24772608 | tf_op jit(solution)/shard_map/pallas_call | solution.py:44
  163.6 0.0 reduce-scatter.2.cloned.1.call-update
  163.6 673.2 %reduce-scatter.2.cloned.1.call-done = f32[128,256]{1,0:T(8,128)} async-done(((f32[16384,256]{1,0:T(8,128)}), f32[128,256]{1,0:T(8,128)}) %reduce-scatter.2.cloned.1.call-update) | async-done | bytes 131088 | tf_op jit(solution)/shard_map/reduce_scatter | solution.py:85
  836.8 0.0 copy-done.1
  836.8 0.0 copy-done.2
  836.8 1.8 bitcast_subtract_fusion
  (3 shorter events, 0.0 us)
Async XLA Ops:
  7.2 3.3 copy-start
  7.2 99.5 %all-gather.3.cloned.1.call-start = ((), (), s32[]{:S(2)}) async-start(), calls=%async_computation.2 | async-start | bytes 25362432 | tf_op jit(solution)/shard_map/all_gather | solution.py:81
  9.0 827.8 %reduce-scatter.2.cloned.1.call-start = ((), (), s32[]{:S(2)}) async-start(), calls=%async_computation.1 | async-start | bytes 16908288 | tf_op jit(solution)/shard_map/reduce_scatter | solution.py:85
  114.5 722.3 %copy-start.1 = (f32[128,256]{1,0:T(8,128)S(1)}, f32[128,256]{1,0:T(8,128)}, u32[]{:S(2)}) copy-start(f32[128,256]{1,0:T(8,128)} %param.12) | copy-start | bytes 393220
  114.5 722.3 %copy-start.2 = (f32[128,256]{1,0:T(8,128)S(1)}, f32[128,256]{1,0:T(8,128)}, u32[]{:S(2)}) copy-start(f32[128,256]{1,0:T(8,128)} %param.13) | copy-start | bytes 393220
Sparse Core Ops, SparseCore 0:
  11.1 95.5 all-gather.2
  163.8 672.9 reduce-scatter.1

commit v2 on v1

v2 whole, which is shorter than its diff:
```python
import functools

import jax
import jax.numpy as jnp
from jax import lax
from jax.experimental import pallas as pl
from jax.experimental.pallas import tpu as pltpu
from jax.sharding import PartitionSpec as P

AXES = ("blk", "grp")
MESH = pl.DeviceIdType.MESH
RING = 4
ORDERS = ((0, 1, 2), (1, 2, 0), (2, 0, 1))


class Place:
    def __init__(self):
        blk = lax.axis_index("blk")
        self.coord = [lax.div(blk, 8), lax.rem(lax.div(blk, 2), 4), lax.axis_index("grp")]
        self.core = lax.rem(blk, 2)

    @staticmethod
    def device(coord, core):
        return (coord[0] * 8 + coord[1] * 2 + core, coord[2])

    def partner(self):
        return self.device(self.coord, 1 - self.core)

    def along(self, axis, step):
        return lax.rem(self.coord[axis] + (RING + step), RING)

    def neighbour(self, axis, step):
        coord = list(self.coord)
        coord[axis] = self.along(axis, step)
        return self.device(coord, self.core)

    def greet(self):
        barrier = pltpu.get_barrier_semaphore()
        peers = [self.neighbour(axis, step) for axis in range(3) for step in (1, -1)]
        for peer in peers + [self.partner()]:
            pl.semaphore_signal(barrier, inc=1, device_id=peer, device_id_type=MESH)
        pl.semaphore_wait(barrier, 7)


def remote(src, dst, send, recv, device):
    return pltpu.make_async_remote_copy(
        src_ref=src, dst_ref=dst, send_sem=send, recv_sem=recv, device_id=device, device_id_type=MESH
    )


def gather_kernel(own_ref, table_ref, cast_ref, local_sem, own_sem, send, recv, pair_send, pair_recv):
    place = Place()
    x, y, z = place.coord
    core = place.core
    other = 1 - core
    half_rows = cast_ref.shape[1] // 2

    def region(part, stage, value, half, side):
        index = list(place.coord)
        for axis in ORDERS[part][:stage]:
            index[axis] = slice(None)
        index[ORDERS[part][stage]] = value
        return table_ref.at[
            index[0], index[1], side, index[2], part, half * half_rows : (half + 1) * half_rows
        ]

    def arrived(part, stage, way, k, side):
        axis = ORDERS[part][stage]
        step = -1 if way == 0 else 1
        value = place.along(axis, step if k < 2 else 2)
        return region(part, stage, value, way if k != 1 else 1 - way, side)

    def outgoing(part, stage, way, k):
        axis = ORDERS[part][stage]
        half = way if k != 1 else 1 - way
        if k < 2:
            dst = region(part, stage, place.coord[axis], half, core)
            src = dst
            if stage == 0:
                src = cast_ref.at[part, half * half_rows : (half + 1) * half_rows]
        else:
            dst = src = arrived(part, stage, way, 0, core)
        device = place.neighbour(axis, 1 if way == 0 else -1)
        return remote(src, dst, send.at[part, stage, way, k], recv.at[part, stage, way, k], device)

    def incoming(part, stage, way, k):
        ref = arrived(part, stage, way, k, core)
        axis = ORDERS[part][stage]
        device = place.neighbour(axis, 1 if way == 0 else -1)
        return remote(ref, ref, send.at[part, stage, way, k], recv.at[part, stage, way, k], device)

    def across(part, stage, way, k, side):
        ref = arrived(part, stage, way, k, side)
        at = (part, stage, way, k)
        return remote(ref, ref, pair_send.at[at], pair_recv.at[at], place.partner())

    cast_ref[...] = own_ref[...].astype(cast_ref.dtype)
    place.greet()
    steps = [(part, way) for part in range(3) for way in range(2)]
    for k in range(2):
        for part, way in steps:
            outgoing(part, 0, way, k).start()
    mine = pltpu.make_async_copy(cast_ref, table_ref.at[x, y, core, z], local_sem)
    mine.start()
    own = remote(cast_ref, table_ref.at[x, y, core, z], own_sem.at[0], own_sem.at[1], place.partner())
    own.start()
    mine.wait()
    for stage in range(3):
        for k in range(3):
            for part in range(3):
                for way in range(2):
                    incoming(part, stage, way, k).wait_recv()
                    if k == 0:
                        outgoing(part, stage, way, 2).start()
                    across(part, stage, way, k, core).start()
                if k == 2 and stage < 2:
                    for way in range(2):
                        outgoing(part, stage + 1, way, 0).start()
                        outgoing(part, stage + 1, way, 1).start()
    own.wait_send()
    theirs = table_ref.at[x, y, other, z]
    remote(theirs, theirs, own_sem.at[0], own_sem.at[1], place.partner()).wait_recv()
    for stage in range(3):
        for k in range(3):
            for part, way in steps:
                outgoing(part, stage, way, k).wait_send()
                across(part, stage, way, k, core).wait_send()
                across(part, stage, way, k, other).wait_recv()


def gather_rows(factors):
    modes, rows, rank = factors.shape
    return pl.pallas_call(
        gather_kernel,
        out_shape=jax.ShapeDtypeStruct((4, 4, 2, 4, modes, rows, rank), jnp.bfloat16),
        in_specs=[pl.BlockSpec(memory_space=pltpu.VMEM)],
        out_specs=pl.BlockSpec(memory_space=pl.ANY),
        scratch_shapes=[
            pltpu.VMEM((modes, rows, rank), jnp.bfloat16),
            pltpu.SemaphoreType.DMA,
            pltpu.SemaphoreType.DMA((2,)),
            pltpu.SemaphoreType.DMA((3, 3, 2, 3)),
            pltpu.SemaphoreType.DMA((3, 3, 2, 3)),
            pltpu.SemaphoreType.DMA((3, 3, 2, 3)),
            pltpu.SemaphoreType.DMA((3, 3, 2, 3)),
        ],
        compiler_params=pltpu.CompilerParams(collective_id=0, has_side_effects=True),
    )(factors)


def block_kernel(slots, edge, chunk, coords_ref, owner_ref, count_ref, block_ref, a_ref, b_ref, c_ref, out_ref, slot_ref):
    slot = pl.program_id(0)

    @pl.when(slot == 0)
    def _():
        @pl.loop(0, slot_ref.shape[0])
        def _(p):
            slot_ref[p] = slots

        @pl.loop(0, slots)
        def _(s):
            slot_ref[owner_ref[0, coords_ref[0, s]]] = s

    @pl.when(slot < count_ref[0])
    def _():
        half_a = a_ref[0] * jnp.bfloat16(0.5)
        rows_c = c_ref[0]
        rank = rows_c.shape[1]
        total = jnp.zeros((edge, rank), jnp.float32)
        for step in range(edge // chunk):
            pair = jnp.concatenate(
                [b_ref[0, pl.ds(step * chunk + j, 1), :] * rows_c for j in range(chunk)], axis=0
            )
            model = lax.dot_general(
                half_a, pair, (((1,), (1,)), ((), ())), preferred_element_type=jnp.float32
            )
            width = chunk * edge
            observed = block_ref[0, :, step * width : (step + 1) * width].astype(jnp.float32)
            resid = (0.5 * jnp.tanh(model) + (0.5 - observed)).astype(jnp.bfloat16)
            total = total + jnp.dot(resid, pair, preferred_element_type=jnp.float32)
        out_ref[0] = total

    @pl.when(slot >= count_ref[0])
    def _():
        out_ref[...] = jnp.zeros_like(out_ref)


def block_gradients(tensor_blocks, table, coords, owner, count, positions, local_blocks):
    slots, edge, merged = tensor_blocks.shape
    modes, _ = coords.shape
    rank = table.shape[2]

    def rows_of(m):
        def index(s, coords_ref, owner_ref, count_ref):
            pos = owner_ref[m, coords_ref[m, jnp.minimum(s, slots - 1)]]
            device = lax.div(pos, local_blocks)
            return ((device * modes + m) * local_blocks + lax.rem(pos, local_blocks), 0, 0)

        return pl.BlockSpec((1, edge, rank), index)

    return pl.pallas_call(
        functools.partial(block_kernel, slots, edge, 8),
        out_shape=(
            jax.ShapeDtypeStruct((slots + 1, edge, rank), jnp.float32),
            jax.ShapeDtypeStruct((positions,), jnp.int32),
        ),
        grid_spec=pltpu.PrefetchScalarGridSpec(
            num_scalar_prefetch=3,
            grid=(slots + 1,),
            in_specs=[
                pl.BlockSpec((1, edge, merged), lambda s, *_: (jnp.minimum(s, slots - 1), 0, 0)),
                rows_of(0),
                rows_of(1),
                rows_of(2),
            ],
            out_specs=(
                pl.BlockSpec((1, edge, rank), lambda s, *_: (s, 0, 0)),
                pl.BlockSpec(memory_space=pltpu.SMEM),
            ),
        ),
        compiler_params=pltpu.CompilerParams(
            dimension_semantics=("arbitrary",), vmem_limit_bytes=48 << 20
        ),
        cost_estimate=pl.CostEstimate(
            flops=4 * slots * edge * merged * rank,
            bytes_accessed=2 * slots * edge * (merged + 5 * rank),
            transcendentals=slots * edge * merged,
        ),
    )(coords, owner, count, tensor_blocks, table, table, table)


CUTS = (((0, 88), (0, 128)), ((0, 88), (128, 256)), ((88, 128), (0, 256)))
SPLITS = ((48, 40), (48, 40), (24, 16))


def half_shape(part, stage):
    (r0, r1), (c0, c1) = CUTS[part]
    sizes = [RING, RING, RING]
    for axis in ORDERS[part][: stage + 1]:
        sizes[axis] = None
    if stage < 2:
        sizes[ORDERS[part][stage + 1]] = 2
        rows = r1 - r0
    else:
        rows = SPLITS[part][0]
    return tuple(n for n in sizes if n is not None) + (rows, c1 - c0)


def scatter_kernel(slot_ref, parts_ref, grad_ref, acc, outbox, inbox, *rest):
    buffers = rest[:9]
    send, recv, pair_send, pair_recv = rest[9:]
    place = Place()
    edge = parts_ref.shape[1]

    def region(ref, part, stage, k, half):
        order = ORDERS[part]
        (r0, r1), (c0, c1) = CUTS[part]
        index = [slice(None)] * 3
        for axis in order[:stage]:
            index[axis] = 0
        index[order[stage]] = k
        if half is not None:
            if stage < 2:
                index[order[stage + 1]] = slice(2 * half, 2 * half + 2)
            else:
                cut = r0 + SPLITS[part][0]
                r0, r1 = (r0, cut) if half == 0 else (cut, r1)
        return ref.at[index[0], index[1], index[2], r0:r1, c0:c1]

    def half_of(way, k):
        return way if k != 1 else 1 - way

    def landing(part, stage, way, k):
        ref = buffers[part * 3 + stage].at[way, k]
        if stage == 2:
            ref = ref.at[0 : SPLITS[part][half_of(way, k)]]
        return ref

    def outgoing(part, stage, way, k):
        offset = 2 if k == 0 else (3 if way == 0 else 1)
        src = region(acc, part, stage, offset, half_of(way, k))
        device = place.neighbour(ORDERS[part][stage], -1 if way == 0 else 1)
        at = (part, stage, way, k)
        return remote(src, landing(part, stage, way, k), send.at[at], recv.at[at], device)

    def take(part, stage, way, k):
        outgoing(part, stage, way, k).wait_recv()
        offset = (3 if way == 0 else 1) if k == 0 else 0
        target = region(acc, part, stage, offset, half_of(way, k))
        target[...] = target[...] + landing(part, stage, way, k)[...]

    def across(part, k):
        at = (part, k)
        return remote(
            region(outbox, part, 0, k, None),
            region(inbox, part, 0, k, None),
            pair_send.at[at],
            pair_recv.at[at],
            place.partner(),
        )

    def take_across(part, k):
        across(part, k).wait_recv()
        target = region(acc, part, 0, k, None)
        target[...] = target[...] + region(inbox, part, 0, k, None)[...]

    def spread(ref, core):
        @pl.loop(0, RING**3)
        def _(r):
            step = (lax.div(r, 16), lax.rem(lax.div(r, 4), 4), lax.rem(r, 4))
            blk, grp = place.device(
                [lax.rem(v + s, RING) for v, s in zip(place.coord, step)], core
            )
            first = (blk * 4 + grp) * 2
            for j in range(2):
                ref[step[0], step[1], step[2], j * edge : (j + 1) * edge, :] = parts_ref[
                    slot_ref[first + j]
                ]

    spread(outbox, 1 - place.core)
    place.greet()
    for k in (2, 3, 1, 0):
        for part in range(3):
            across(part, k).start()
    spread(acc, place.core)
    for part in range(3):
        take_across(part, 2)
        for way in range(2):
            outgoing(part, 0, way, 0).start()
    for part in range(3):
        for way, k in ((0, 3), (1, 1)):
            take_across(part, k)
            outgoing(part, 0, way, 1).start()
    for stage in range(3):
        for part in range(3):
            for way in range(2):
                take(part, stage, way, 0)
                outgoing(part, stage, way, 2).start()
        if stage == 0:
            for part in range(3):
                take_across(part, 0)
        for part in range(3):
            for k in (1, 2):
                for way in range(2):
                    take(part, stage, way, k)
            if stage < 2:
                for k in range(2):
                    for way in range(2):
                        outgoing(part, stage + 1, way, k).start()
    grad_ref[...] = acc[0, 0, 0]
    for part in range(3):
        for k in range(4):
            across(part, k).wait_send()
        for stage in range(3):
            for way in range(2):
                for k in range(3):
                    outgoing(part, stage, way, k).wait_send()


def scatter_gradients(parts, slot_of):
    edge, rank = parts.shape[1:]
    dense = (RING, RING, RING, 2 * edge, rank)
    buffers = [
        pltpu.VMEM((2, 3) + half_shape(part, stage), jnp.float32)
        for part in range(3)
        for stage in range(3)
    ]
    return pl.pallas_call(
        scatter_kernel,
        out_shape=jax.ShapeDtypeStruct((2 * edge, rank), jnp.float32),
        in_specs=[
            pl.BlockSpec(memory_space=pltpu.SMEM),
            pl.BlockSpec(memory_space=pltpu.VMEM),
        ],
        out_specs=pl.BlockSpec(memory_space=pltpu.VMEM),
        scratch_shapes=[pltpu.VMEM(dense, jnp.float32)] * 3
        + buffers
        + [
            pltpu.SemaphoreType.DMA((3, 3, 2, 3)),
            pltpu.SemaphoreType.DMA((3, 3, 2, 3)),
            pltpu.SemaphoreType.DMA((3, 4)),
            pltpu.SemaphoreType.DMA((3, 4)),
        ],
        compiler_params=pltpu.CompilerParams(
            collective_id=1, has_side_effects=True, vmem_limit_bytes=56 << 20
        ),
    )(slot_of, parts)


def per_device(tensor_blocks, block_coords, block_count, row_owner, factors, moment1, moment2):
    edge = tensor_blocks.shape[1]
    modes, local_rows, rank = factors.shape
    local_blocks = local_rows // edge
    positions = lax.axis_size(AXES) * local_blocks
    table = gather_rows(factors).reshape(modes * positions, edge, rank)
    parts, slot_of = block_gradients(
        tensor_blocks, table, block_coords, row_owner, block_count, positions, local_blocks
    )
    grad = scatter_gradients(parts, slot_of)
    new_moment1 = 0.9 * moment1 + 0.1 * grad
    new_moment2 = 0.999 * moment2 + 0.001 * grad * grad
    new_factor = factors[0] - 0.02 * (new_moment1 / (1.0 - 0.9**8)) / (
        jnp.sqrt(new_moment2 / (1.0 - 0.999**8)) + 1e-08
    )
    return (new_factor, new_moment1, new_moment2)


def solution(mesh):
    return jax.shard_map(
        per_device,
        mesh=mesh,
        in_specs=(
            P(AXES, None, None),
            P(None, AXES),
            P(AXES),
            P(),
            P(None, AXES, None),
            P(AXES, None),
            P(AXES, None),
        ),
        out_specs=(P(AXES, None), P(AXES, None), P(AXES, None)),
        check_vma=False,
    )
```

time: 846 us -> 183 us (0.22)
  waiting for transfers between devices: 767 us -> 0 us
  Pallas kernels: 49.1 us -> 177 us
  between operations: 14.7 us -> 1.39 us
    reduce_scatter x1 -> x0, waiting for transfers between devices: 673 us -> none  [per_device(): lax.psum_scatter(parts.reshape(blocks * edge, rank), AXES, scatter_dimens...]
    pallas_call x1 -> x3, Pallas kernels: 49.1 us -> 177 us  [the longest x1 66.4 us: gather_rows(): pl.pallas_call(gather_kernel, out_shape=jax.ShapeDtypeStruct((4, 4, 2, 4,...]
    all_gather x1 -> x0, waiting for transfers between devices: 93.3 us -> none  [per_device(): lax.all_gather(factors.astype(jnp.bfloat16), AXES, axis=0, tiled=False)]
  transfers between devices with their start and end apart: 2 -> 0, of which waited for: 2 -> 0; matrix products, arithmetic and copies ran while one was open for 0% -> 0% of each run, Pallas kernels for 0% -> 0%
where the time goes in v2:
time: 183 us; the launch traced here: 182 us
  Pallas kernels  177 us (97%)
  local copies, waits for them, and re-layouts  2 us (1%)
    pallas_call x1, Pallas kernels, gather_rows(): pl.pallas_call(gather_kernel, out_shape=jax.ShapeDtypeStruct((4, 4, 2, 4,...  66.4 us
    pallas_call x1, Pallas kernels, scatter_gradients(): pl.pallas_call(scatter_kernel, out_shape=jax.ShapeDtypeStruct((2 * edge,...  57.7 us
    pallas_call x1, Pallas kernels, block_gradients(): pl.pallas_call(functools.partial(block_kernel, slots, edge, 8), out_shape...  53.1 us

profile of v2, /device:TPU:0, one launch (start us, length us, event | category | flops | bytes accessed | tf_op | source)
XLA Modules:
  0.0 182.3 jit_solution(8563893915446483870)
XLA Ops:
  0.6 0.0 copy-start.1
  0.6 0.0 copy-start.2
  1.3 66.4 %shard_map.94 = bf16[4,4,2,4,3,128,256]{6,5,4,3,2,1,0:T(8,128)(2,1)} custom-call(f32[3,128,256]{2,1,0:T(8,128)} %own_ref.1), custom_call_target="tpu_custom_call" | custom-call | tf_op jit(solution)/shard_map/pallas_call | solution.py:133
  67.7 0.0 copy-done.1
  67.7 0.0 copy-done.2
  67.7 0.0 copy-start.4
  67.7 0.0 copy-start.5
  67.8 53.1 %shard_map.95 = (f32[37,64,256]{2,1,0:T(8,128)S(1)}, s32[256]{0:T(256)S(1)}) custom-call(s32[3,36]{1,0:T(4,128)S(1)} %copy-done.2, s32[3,256]{1,0:T(4,128)S(1)} %copy-done.1, s32[1]{0:T(128)S(6)} %copy.10.count_ref, bf16[36,64,4096]{2,1,0:T(8,128)(2,1)} %block_ref.1, bf16[768,64,256]{2,1,0:T(8,128)(2,1)} %bitcast.3, bf16[768,64,256]{2,1,0:T(8,128)(2,1)} %bitcast.4, ...), custom_call_target="tpu_custom_call" | custom-call | flops 9663676416 | bytes 24772608 | tf_op jit(solution)/shard_map/pallas_call | solution.py:201
  120.9 0.0 copy-start
  120.9 1.4 copy-done
  122.3 0.0 copy-start.3
  122.3 0.6 copy-done.3
  122.9 57.7 %shard_map.96 = f32[128,256]{1,0:T(8,128)} custom-call(s32[256]{0:T(256)} %copy-done.3, f32[37,64,256]{2,1,0:T(8,128)} %copy-done), custom_call_target="tpu_custom_call" | custom-call | tf_op jit(solution)/shard_map/pallas_call | solution.py:368
  180.6 0.0 copy-done.4
  180.6 0.0 copy-done.5
  180.6 1.8 bitcast_subtract_fusion
Async XLA Ops:
  0.6 67.1 %copy-start.1 = (s32[3,256]{1,0:T(4,128)S(1)}, s32[3,256]{1,0:T(4,128)}, u32[]{:S(2)}) copy-start(s32[3,256]{1,0:T(4,128)} %owner_ref.1) | copy-start | bytes 9220
  0.6 67.1 %copy-start.2 = (s32[3,36]{1,0:T(4,128)S(1)}, s32[3,36]{1,0:T(4,128)}, u32[]{:S(2)}) copy-start(s32[3,36]{1,0:T(4,128)} %coords_ref.1) | copy-start | bytes 1300
  67.7 112.8 %copy-start.4 = (f32[128,256]{1,0:T(8,128)S(1)}, f32[128,256]{1,0:T(8,128)}, u32[]{:S(2)}) copy-start(f32[128,256]{1,0:T(8,128)} %param.12) | copy-start | bytes 393220
  67.7 112.8 %copy-start.5 = (f32[128,256]{1,0:T(8,128)S(1)}, f32[128,256]{1,0:T(8,128)}, u32[]{:S(2)}) copy-start(f32[128,256]{1,0:T(8,128)} %param.13) | copy-start | bytes 393220
  120.9 1.4 copy-start
  122.3 0.6 copy-start.3

commit v3 on v2

--- a/solution.py
+++ b/solution.py
@@ -148,85 +148,127 @@
     )(factors)
 
 
-def block_kernel(slots, edge, chunk, coords_ref, owner_ref, count_ref, block_ref, a_ref, b_ref, c_ref, out_ref, slot_ref):
-    slot = pl.program_id(0)
-
-    @pl.when(slot == 0)
+def block_part(edge, chunk, half_a, b_ref, rows_c, block_ref):
+    total = jnp.zeros((edge, rows_c.shape[1]), jnp.float32)
+    width = chunk * edge
+    for step in range(edge // chunk):
+        pair = jnp.concatenate(
+            [b_ref[pl.ds(step * chunk + j, 1), :] * rows_c for j in range(chunk)], axis=0
+        )
+        model = lax.dot_general(
+            half_a, pair, (((1,), (1,)), ((), ())), preferred_element_type=jnp.float32
+        )
+        observed = block_ref[:, step * width : (step + 1) * width].astype(jnp.float32)
+        resid = (0.5 * jnp.tanh(model) + (0.5 - observed)).astype(jnp.bfloat16)
+        total = total + jnp.dot(resid, pair, preferred_element_type=jnp.float32)
+    return total
+
+
+def block_kernel(
+    local_blocks, coords_ref, owner_ref, count_ref, blocks_ref, table_ref, parts_ref, slot_ref,
+    block_buf, rows_buf, part_buf, sems, part_sems,
+):
+    slots, edge, _ = blocks_ref.shape
+    depth = block_buf.shape[0]
+    modes = rows_buf.shape[1]
+    count = count_ref[0]
+
+    def copies(s):
+        at = lax.rem(s, depth)
+        made = [pltpu.make_async_copy(blocks_ref.at[s], block_buf.at[at], sems.at[at, modes])]
+        for m in range(modes):
+            pos = owner_ref[m, coords_ref[m, s]]
+            row = (lax.div(pos, local_blocks) * modes + m) * local_blocks + lax.rem(pos, local_blocks)
+            made.append(
+                pltpu.make_async_copy(table_ref.at[row], rows_buf.at[at, m], sems.at[at, m])
+            )
+        return made
+
+    def fetch(s):
+        @pl.when(s < count)
+        def _():
+            for copy in copies(s):
+                copy.start()
+
+    for s in range(depth - 2):
+        fetch(s)
+
+    @pl.loop(0, slot_ref.shape[0])
+    def _(p):
+        slot_ref[p] = slots
+
+    @pl.loop(0, count)
+    def _(s):
+        slot_ref[owner_ref[0, coords_ref[0, s]]] = s
+
+    def store(s):
+        return pltpu.make_async_copy(part_buf.at[s], parts_ref.at[s], part_sems.at[s])
+
+    part_buf[slots] = jnp.zeros(part_buf.shape[1:], jnp.float32)
+    store(slots).start()
+
+    def compute(s):
+        at = lax.rem(s, depth)
+        half_a = rows_buf[at, 0] * jnp.bfloat16(0.5)
+        part_buf[s] = block_part(
+            edge, 16, half_a, rows_buf.at[at, 1], rows_buf[at, 2], block_buf.at[at]
+        )
+        store(s).start()
+
+    pairs = lax.div(count, 2)
+
+    @pl.loop(0, pairs)
+    def _(h):
+        for q in range(2):
+            fetch(2 * h + depth - 2 + q)
+        for q in range(2):
+            for copy in copies(2 * h + q):
+                copy.wait()
+        for q in range(2):
+            compute(2 * h + q)
+
+    @pl.when(2 * pairs < count)
     def _():
-        @pl.loop(0, slot_ref.shape[0])
-        def _(p):
-            slot_ref[p] = slots
-
-        @pl.loop(0, slots)
-        def _(s):
-            slot_ref[owner_ref[0, coords_ref[0, s]]] = s
-
-    @pl.when(slot < count_ref[0])
-    def _():
-        half_a = a_ref[0] * jnp.bfloat16(0.5)
-        rows_c = c_ref[0]
-        rank = rows_c.shape[1]
-        total = jnp.zeros((edge, rank), jnp.float32)
-        for step in range(edge // chunk):
-            pair = jnp.concatenate(
-                [b_ref[0, pl.ds(step * chunk + j, 1), :] * rows_c for j in range(chunk)], axis=0
-            )
-            model = lax.dot_general(
-                half_a, pair, (((1,), (1,)), ((), ())), preferred_element_type=jnp.float32
-            )
-            width = chunk * edge
-            observed = block_ref[0, :, step * width : (step + 1) * width].astype(jnp.float32)
-            resid = (0.5 * jnp.tanh(model) + (0.5 - observed)).astype(jnp.bfloat16)
-            total = total + jnp.dot(resid, pair, preferred_element_type=jnp.float32)
-        out_ref[0] = total
-
-    @pl.when(slot >= count_ref[0])
-    def _():
-        out_ref[...] = jnp.zeros_like(out_ref)
+        for copy in copies(2 * pairs):
+            copy.wait()
+        compute(2 * pairs)
+
+    @pl.loop(0, count)
+    def _(s):
+        store(s).wait()
+
+    store(slots).wait()
 
 
 def block_gradients(tensor_blocks, table, coords, owner, count, positions, local_blocks):
     slots, edge, merged = tensor_blocks.shape
     modes, _ = coords.shape
     rank = table.shape[2]
-
-    def rows_of(m):
-        def index(s, coords_ref, owner_ref, count_ref):
-            pos = owner_ref[m, coords_ref[m, jnp.minimum(s, slots - 1)]]
-            device = lax.div(pos, local_blocks)
-            return ((device * modes + m) * local_blocks + lax.rem(pos, local_blocks), 0, 0)
-
-        return pl.BlockSpec((1, edge, rank), index)
-
+    depth = 6
+    smem = pl.BlockSpec(memory_space=pltpu.SMEM)
+    far = pl.BlockSpec(memory_space=pltpu.HBM)
     return pl.pallas_call(
-        functools.partial(block_kernel, slots, edge, 8),
+        functools.partial(block_kernel, local_blocks),
         out_shape=(
             jax.ShapeDtypeStruct((slots + 1, edge, rank), jnp.float32),
             jax.ShapeDtypeStruct((positions,), jnp.int32),
         ),
-        grid_spec=pltpu.PrefetchScalarGridSpec(
-            num_scalar_prefetch=3,
-            grid=(slots + 1,),
-            in_specs=[
-                pl.BlockSpec((1, edge, merged), lambda s, *_: (jnp.minimum(s, slots - 1), 0, 0)),
-                rows_of(0),
-                rows_of(1),
-                rows_of(2),
-            ],
-            out_specs=(
-                pl.BlockSpec((1, edge, rank), lambda s, *_: (s, 0, 0)),
-                pl.BlockSpec(memory_space=pltpu.SMEM),
-            ),
-        ),
-        compiler_params=pltpu.CompilerParams(
-            dimension_semantics=("arbitrary",), vmem_limit_bytes=48 << 20
-        ),
+        in_specs=[smem, smem, smem, far, far],
+        out_specs=(far, smem),
+        scratch_shapes=[
+            pltpu.VMEM((depth, edge, merged), jnp.bfloat16),
+            pltpu.VMEM((depth, modes, edge, rank), jnp.bfloat16),
+            pltpu.VMEM((slots + 1, edge, rank), jnp.float32),
+            pltpu.SemaphoreType.DMA((depth, modes + 1)),
+            pltpu.SemaphoreType.DMA((slots + 1,)),
+        ],
+        compiler_params=pltpu.CompilerParams(vmem_limit_bytes=62 << 20),
         cost_estimate=pl.CostEstimate(
             flops=4 * slots * edge * merged * rank,
             bytes_accessed=2 * slots * edge * (merged + 5 * rank),
             transcendentals=slots * edge * merged,
         ),
-    )(coords, owner, count, tensor_blocks, table, table, table)
+    )(coords, owner, count, tensor_blocks, table)
 
 
 CUTS = (((0, 88), (0, 128)), ((0, 88), (128, 256)), ((88, 128), (0, 256)))
@@ -382,7 +424,7 @@
             pltpu.SemaphoreType.DMA((3, 4)),
         ],
         compiler_params=pltpu.CompilerParams(
-            collective_id=1, has_side_effects=True, vmem_limit_bytes=56 << 20
+            collective_id=1, has_side_effects=True, vmem_limit_bytes=62 << 20
         ),
     )(slot_of, parts)
 

time: 183 us -> 166 us (0.907)
  Pallas kernels: 177 us -> 163 us
  local copies, waits for them, and re-layouts: 2 us -> 0.01 us
    pallas_call x1, Pallas kernels: 53.1 us -> 44 us  [block_gradients(): pl.pallas_call(functools.partial(block_kernel, local_blocks), out_shape=(...]
    pallas_call x1, Pallas kernels: 57.7 us -> 52.4 us  [scatter_gradients(): pl.pallas_call(scatter_kernel, out_shape=jax.ShapeDtypeStruct((2 * edge,...]
    unnamed x12 -> x4, local copies, waits for them, and re-layouts: 2 us -> 0.01 us
where the time goes in v3:
time: 166 us
  Pallas kernels  163 us (98%)
  other arithmetic  1.75 us (1%)
    pallas_call x1, Pallas kernels, gather_rows(): pl.pallas_call(gather_kernel, out_shape=jax.ShapeDtypeStruct((4, 4, 2, 4,...  66.4 us
    pallas_call x1, Pallas kernels, scatter_gradients(): pl.pallas_call(scatter_kernel, out_shape=jax.ShapeDtypeStruct((2 * edge,...  52.4 us
    pallas_call x1, Pallas kernels, block_gradients(): pl.pallas_call(functools.partial(block_kernel, local_blocks), out_shape=(...  44 us

profile of v3, /device:TPU:0, one launch (start us, length us, event | category | flops | bytes accessed | tf_op | source)
XLA Modules:
  0.0 165.9 jit_solution(9874255758374913853)
XLA Ops:
  1.3 66.4 %shard_map.94 = bf16[4,4,2,4,3,128,256]{6,5,4,3,2,1,0:T(8,128)(2,1)} custom-call(f32[3,128,256]{2,1,0:T(8,128)} %own_ref.1), custom_call_target="tpu_custom_call" | custom-call | tf_op jit(solution)/shard_map/pallas_call | solution.py:133
  67.7 0.0 copy-start
  67.7 0.0 copy-start.1
  67.7 44.0 %shard_map.95 = (f32[37,64,256]{2,1,0:T(8,128)}, s32[256]{0:T(256)}) custom-call(s32[3,36]{1,0:T(4,128)} %coords_ref.1, s32[3,256]{1,0:T(4,128)} %owner_ref.1, s32[1]{0:T(128)S(6)} %copy.10.count_ref, bf16[36,64,4096]{2,1,0:T(8,128)(2,1)} %blocks_ref.1, bf16[768,64,256]{2,1,0:T(8,128)(2,1)} %bitcast.3), custom_call_target="tpu_custom_call" | custom-call | flops 9663676416 | bytes 24772608 | tf_op jit(solution)/shard_map/pallas_call | solution.py:250
  111.7 52.4 %shard_map.96 = f32[128,256]{1,0:T(8,128)} custom-call(s32[256]{0:T(256)} %get-tuple-element.5.slot_ref, f32[37,64,256]{2,1,0:T(8,128)} %get-tuple-element.6.parts_ref), custom_call_target="tpu_custom_call" | custom-call | tf_op jit(solution)/shard_map/pallas_call | solution.py:410
  164.1 0.0 copy-done
  164.1 0.0 copy-done.1
  164.1 1.8 %bitcast_subtract_fusion = (f32[128,256]{1,0:T(8,128)}, f32[128,256]{1,0:T(8,128)}, f32[128,256]{1,0:T(8,128)}) fusion(f32[3,128,256]{2,1,0:T(8,128)} %own_ref.1, f32[128,256]{1,0:T(8,128)} %shard_map.96, f32[128,256]{1,0:T(8,128)S(1)} %copy-done, f32[128,256]{1,0:T(8,128)S(1)} %copy-done.1), kind=kLoop, calls=%fused_computation.2 | loop fusion | flops 393216 | bytes 917504 | tf_op jit(solution)/shard_map/sub | solution.py:444
Async XLA Ops:
  67.7 96.4 %copy-start = (f32[128,256]{1,0:T(8,128)S(1)}, f32[128,256]{1,0:T(8,128)}, u32[]{:S(2)}) copy-start(f32[128,256]{1,0:T(8,128)} %param.12) | copy-start | bytes 393220
  67.7 96.4 %copy-start.1 = (f32[128,256]{1,0:T(8,128)S(1)}, f32[128,256]{1,0:T(8,128)}, u32[]{:S(2)}) copy-start(f32[128,256]{1,0:T(8,128)} %param.13) | copy-start | bytes 393220

commit v4 on v3

--- a/solution.py
+++ b/solution.py
@@ -34,6 +34,13 @@
         coord[axis] = self.along(axis, step)
         return self.device(coord, self.core)
 
+    def offset(self, device):
+        blk = lax.div(device, RING)
+        coord = (lax.div(blk, 8), lax.rem(lax.div(blk, 2), 4), lax.rem(device, RING))
+        steps = [lax.rem(v - me + RING, RING) for v, me in zip(coord, self.coord)]
+        side = lax.rem(lax.rem(blk, 2) + self.core, 2)
+        return ((steps[0] * RING + steps[1]) * RING + steps[2]) * 2 + side
+
     def greet(self):
         barrier = pltpu.get_barrier_semaphore()
         peers = [self.neighbour(axis, step) for axis in range(3) for step in (1, -1)]
@@ -48,101 +55,145 @@
     )
 
 
+ALL = slice(0, RING)
+FAR = slice(1, RING)
+GROUPS = (
+    ((),),
+    ((0,), (FAR,)),
+    ((0, 0), (FAR, 0), (ALL, 1), (ALL, 3), (ALL, 2)),
+)
+LISTED = [(stage, g) for stage in range(3) for g in range(len(GROUPS[stage]))]
+NUMBER = {at: i for i, at in enumerate(LISTED)}
+
+
 def gather_kernel(own_ref, table_ref, cast_ref, local_sem, own_sem, send, recv, pair_send, pair_recv):
     place = Place()
-    x, y, z = place.coord
-    core = place.core
-    other = 1 - core
     half_rows = cast_ref.shape[1] // 2
 
-    def region(part, stage, value, half, side):
-        index = list(place.coord)
-        for axis in ORDERS[part][:stage]:
-            index[axis] = slice(None)
+    def region(part, stage, g, value, half, side):
+        index = [0, 0, 0]
+        for axis, piece in zip(ORDERS[part], GROUPS[stage][g]):
+            index[axis] = piece
         index[ORDERS[part][stage]] = value
-        return table_ref.at[
-            index[0], index[1], side, index[2], part, half * half_rows : (half + 1) * half_rows
-        ]
-
-    def arrived(part, stage, way, k, side):
-        axis = ORDERS[part][stage]
-        step = -1 if way == 0 else 1
-        value = place.along(axis, step if k < 2 else 2)
-        return region(part, stage, value, way if k != 1 else 1 - way, side)
-
-    def outgoing(part, stage, way, k):
-        axis = ORDERS[part][stage]
-        half = way if k != 1 else 1 - way
-        if k < 2:
-            dst = region(part, stage, place.coord[axis], half, core)
-            src = dst
-            if stage == 0:
+        rows = slice(0, 2 * half_rows) if half is None else slice(half * half_rows, (half + 1) * half_rows)
+        return table_ref.at[index[0], index[1], index[2], side, part, rows]
+
+    def half_of(way, k):
+        return way if k != 1 else 1 - way
+
+    def copy(part, stage, g, way, k):
+        half = half_of(way, k)
+        came = 3 if way == 0 else 1
+        if k == 2:
+            src = region(part, stage, g, came, half, 0)
+            dst = region(part, stage, g, 2, half, 0)
+        else:
+            src = region(part, stage, g, 0, half, 0)
+            dst = region(part, stage, g, came, half, 0)
+            if g == 0:
                 src = cast_ref.at[part, half * half_rows : (half + 1) * half_rows]
-        else:
-            dst = src = arrived(part, stage, way, 0, core)
-        device = place.neighbour(axis, 1 if way == 0 else -1)
-        return remote(src, dst, send.at[part, stage, way, k], recv.at[part, stage, way, k], device)
-
-    def incoming(part, stage, way, k):
-        ref = arrived(part, stage, way, k, core)
-        axis = ORDERS[part][stage]
-        device = place.neighbour(axis, 1 if way == 0 else -1)
-        return remote(ref, ref, send.at[part, stage, way, k], recv.at[part, stage, way, k], device)
-
-    def across(part, stage, way, k, side):
-        ref = arrived(part, stage, way, k, side)
-        at = (part, stage, way, k)
-        return remote(ref, ref, pair_send.at[at], pair_recv.at[at], place.partner())
+        device = place.neighbour(ORDERS[part][stage], 1 if way == 0 else -1)
+        at = (part, NUMBER[stage, g], way, k)
+        return remote(src, dst, send.at[at], recv.at[at], device)
+
+    def across(part, stage, g, way, j):
+        value, half = ((3 if way == 0 else 1), None) if j == 0 else (2, way)
+        at = (part, NUMBER[stage, g], way, j)
+        return remote(
+            region(part, stage, g, value, half, 0),
+            region(part, stage, g, value, half, 1),
+            pair_send.at[at],
+            pair_recv.at[at],
+            place.partner(),
+        )
+
+    steps = [(part, way) for part in range(3) for way in range(2)]
+
+    def begin(stage, g):
+        for k in range(2):
+            for part, way in steps:
+                copy(part, stage, g, way, k).start()
+
+    def arrive(stage, g, k):
+        for part, way in steps:
+            copy(part, stage, g, way, k).wait_recv()
+            if k == 0:
+                copy(part, stage, g, way, 2).start()
+            else:
+                across(part, stage, g, way, k - 1).start()
+
+    def drain(stage, g):
+        for part, way in steps:
+            for k in range(3):
+                copy(part, stage, g, way, k).wait_send()
+            for j in range(2):
+                across(part, stage, g, way, j).wait_send()
+
+    def collect(stage, g):
+        for part, way in steps:
+            for j in range(2):
+                across(part, stage, g, way, j).wait_recv()
 
     cast_ref[...] = own_ref[...].astype(cast_ref.dtype)
     place.greet()
-    steps = [(part, way) for part in range(3) for way in range(2)]
-    for k in range(2):
-        for part, way in steps:
-            outgoing(part, 0, way, k).start()
-    mine = pltpu.make_async_copy(cast_ref, table_ref.at[x, y, core, z], local_sem)
+    for stage in range(3):
+        begin(stage, 0)
+    mine = pltpu.make_async_copy(cast_ref, table_ref.at[0, 0, 0, 0], local_sem)
     mine.start()
-    own = remote(cast_ref, table_ref.at[x, y, core, z], own_sem.at[0], own_sem.at[1], place.partner())
+    own = remote(cast_ref, table_ref.at[0, 0, 0, 1], own_sem.at[0], own_sem.at[1], place.partner())
     own.start()
     mine.wait()
-    for stage in range(3):
-        for k in range(3):
-            for part in range(3):
-                for way in range(2):
-                    incoming(part, stage, way, k).wait_recv()
-                    if k == 0:
-                        outgoing(part, stage, way, 2).start()
-                    across(part, stage, way, k, core).start()
-                if k == 2 and stage < 2:
-                    for way in range(2):
-                        outgoing(part, stage + 1, way, 0).start()
-                        outgoing(part, stage + 1, way, 1).start()
-    own.wait_send()
-    theirs = table_ref.at[x, y, other, z]
-    remote(theirs, theirs, own_sem.at[0], own_sem.at[1], place.partner()).wait_recv()
-    for stage in range(3):
-        for k in range(3):
-            for part, way in steps:
-                outgoing(part, stage, way, k).wait_send()
-                across(part, stage, way, k, core).wait_send()
-                across(part, stage, way, k, other).wait_recv()
+    arrive(0, 0, 0)
+    arrive(0, 0, 1)
+    arrive(1, 0, 0)
+    arrive(0, 0, 2)
+    begin(1, 1)
+    begin(2, 1)
+    arrive(2, 0, 0)
+    for k in range(1, 3):
+        arrive(1, 0, k)
+        arrive(2, 0, k)
+    arrive(1, 1, 0)
+    arrive(1, 1, 1)
+    begin(2, 2)
+    begin(2, 3)
+    arrive(2, 1, 0)
+    arrive(1, 1, 2)
+    begin(2, 4)
+    arrive(2, 1, 1)
+    arrive(2, 1, 2)
+    own.wait()
+    for at in ((0, 0), (1, 0), (2, 0), (1, 1)):
+        drain(*at)
+        collect(*at)
+    for g in (2, 3, 4):
+        arrive(2, g, 0)
+        arrive(2, g, 1)
+    drain(2, 1)
+    collect(2, 1)
+    for g in (2, 3, 4):
+        arrive(2, g, 2)
+    for g in (2, 3, 4):
+        drain(2, g)
+        collect(2, g)
 
 
 def gather_rows(factors):
     modes, rows, rank = factors.shape
+    count = len(LISTED)
     return pl.pallas_call(
         gather_kernel,
-        out_shape=jax.ShapeDtypeStruct((4, 4, 2, 4, modes, rows, rank), jnp.bfloat16),
+        out_shape=jax.ShapeDtypeStruct((RING, RING, RING, 2, modes, rows, rank), jnp.bfloat16),
         in_specs=[pl.BlockSpec(memory_space=pltpu.VMEM)],
         out_specs=pl.BlockSpec(memory_space=pl.ANY),
         scratch_shapes=[
             pltpu.VMEM((modes, rows, rank), jnp.bfloat16),
             pltpu.SemaphoreType.DMA,
             pltpu.SemaphoreType.DMA((2,)),
-            pltpu.SemaphoreType.DMA((3, 3, 2, 3)),
-            pltpu.SemaphoreType.DMA((3, 3, 2, 3)),
-            pltpu.SemaphoreType.DMA((3, 3, 2, 3)),
-            pltpu.SemaphoreType.DMA((3, 3, 2, 3)),
+            pltpu.SemaphoreType.DMA((3, count, 2, 3)),
+            pltpu.SemaphoreType.DMA((3, count, 2, 3)),
+            pltpu.SemaphoreType.DMA((3, count, 2, 2)),
+            pltpu.SemaphoreType.DMA((3, count, 2, 2)),
         ],
         compiler_params=pltpu.CompilerParams(collective_id=0, has_side_effects=True),
     )(factors)
@@ -172,13 +223,15 @@
     depth = block_buf.shape[0]
     modes = rows_buf.shape[1]
     count = count_ref[0]
+    place = Place()
 
     def copies(s):
         at = lax.rem(s, depth)
         made = [pltpu.make_async_copy(blocks_ref.at[s], block_buf.at[at], sems.at[at, modes])]
         for m in range(modes):
             pos = owner_ref[m, coords_ref[m, s]]
-            row = (lax.div(pos, local_blocks) * modes + m) * local_blocks + lax.rem(pos, local_blocks)
+            row = (place.offset(lax.div(pos, local_blocks)) * modes + m) * local_blocks
+            row = row + lax.rem(pos, local_blocks)
             made.append(
                 pltpu.make_async_copy(table_ref.at[row], rows_buf.at[at, m], sems.at[at, m])
             )

time: 166 us -> 164 us (0.988)
  Pallas kernels: 163 us -> 161 us
    pallas_call x1, Pallas kernels: 66.4 us -> 62.1 us  [gather_rows(): pl.pallas_call(gather_kernel, out_shape=jax.ShapeDtypeStruct((RING, RING,...]
    pallas_call x1, Pallas kernels: 44 us -> 45.9 us  [block_gradients(): pl.pallas_call(functools.partial(block_kernel, local_blocks), out_shape=(...]
where the time goes in v4:
time: 164 us
  Pallas kernels  161 us (98%)
  other arithmetic  1.75 us (1%)
    pallas_call x1, Pallas kernels, gather_rows(): pl.pallas_call(gather_kernel, out_shape=jax.ShapeDtypeStruct((RING, RING,...  62.1 us
    pallas_call x1, Pallas kernels, scatter_gradients(): pl.pallas_call(scatter_kernel, out_shape=jax.ShapeDtypeStruct((2 * edge,...  52.9 us
    pallas_call x1, Pallas kernels, block_gradients(): pl.pallas_call(functools.partial(block_kernel, local_blocks), out_shape=(...  45.9 us

profile of v4, /device:TPU:0, one launch (start us, length us, event | category | flops | bytes accessed | tf_op | source)
XLA Modules:
  0.0 163.9 jit_solution(7332988156900255351)
XLA Ops:
  1.3 62.1 %shard_map.94 = bf16[4,4,4,2,3,128,256]{6,5,4,3,2,1,0:T(8,128)(2,1)} custom-call(f32[3,128,256]{2,1,0:T(8,128)} %own_ref.1), custom_call_target="tpu_custom_call" | custom-call | tf_op jit(solution)/shard_map/pallas_call | solution.py:184
  63.4 0.0 copy-start
  63.4 0.0 copy-start.1
  63.4 45.9 %shard_map.95 = (f32[37,64,256]{2,1,0:T(8,128)}, s32[256]{0:T(256)}) custom-call(s32[3,36]{1,0:T(4,128)} %coords_ref.1, s32[3,256]{1,0:T(4,128)} %owner_ref.1, s32[1]{0:T(128)S(6)} %copy.10.count_ref, bf16[36,64,4096]{2,1,0:T(8,128)(2,1)} %blocks_ref.1, bf16[768,64,256]{2,1,0:T(8,128)(2,1)} %bitcast.3), custom_call_target="tpu_custom_call" | custom-call | flops 9663676416 | bytes 24772608 | tf_op jit(solution)/shard_map/pallas_call | solution.py:303
  109.3 52.9 %shard_map.96 = f32[128,256]{1,0:T(8,128)} custom-call(s32[256]{0:T(256)} %get-tuple-element.5.slot_ref, f32[37,64,256]{2,1,0:T(8,128)} %get-tuple-element.6.parts_ref), custom_call_target="tpu_custom_call" | custom-call | tf_op jit(solution)/shard_map/pallas_call | solution.py:463
  162.2 0.0 copy-done
  162.2 0.0 copy-done.1
  162.2 1.8 %bitcast_subtract_fusion = (f32[128,256]{1,0:T(8,128)}, f32[128,256]{1,0:T(8,128)}, f32[128,256]{1,0:T(8,128)}) fusion(f32[3,128,256]{2,1,0:T(8,128)} %own_ref.1, f32[128,256]{1,0:T(8,128)} %shard_map.96, f32[128,256]{1,0:T(8,128)S(1)} %copy-done, f32[128,256]{1,0:T(8,128)S(1)} %copy-done.1), kind=kLoop, calls=%fused_computation.2 | loop fusion | flops 393216 | bytes 917504 | tf_op jit(solution)/shard_map/sub | solution.py:497
Async XLA Ops:
  63.4 98.8 %copy-start = (f32[128,256]{1,0:T(8,128)S(1)}, f32[128,256]{1,0:T(8,128)}, u32[]{:S(2)}) copy-start(f32[128,256]{1,0:T(8,128)} %param.12) | copy-start | bytes 393220
  63.4 98.8 %copy-start.1 = (f32[128,256]{1,0:T(8,128)S(1)}, f32[128,256]{1,0:T(8,128)}, u32[]{:S(2)}) copy-start(f32[128,256]{1,0:T(8,128)} %param.13) | copy-start | bytes 393220

commit v5 on v3

--- a/solution.py
+++ b/solution.py
@@ -35,11 +35,17 @@
         return self.device(coord, self.core)
 
     def greet(self):
+        self.announce()
+        self.await_peers()
+
+    def announce(self):
         barrier = pltpu.get_barrier_semaphore()
         peers = [self.neighbour(axis, step) for axis in range(3) for step in (1, -1)]
         for peer in peers + [self.partner()]:
             pl.semaphore_signal(barrier, inc=1, device_id=peer, device_id_type=MESH)
-        pl.semaphore_wait(barrier, 7)
+
+    def await_peers(self):
+        pl.semaphore_wait(pltpu.get_barrier_semaphore(), 7)
 
 
 def remote(src, dst, send, recv, device):
@@ -277,27 +283,29 @@
 
 def half_shape(part, stage):
     (r0, r1), (c0, c1) = CUTS[part]
-    sizes = [RING, RING, RING]
-    for axis in ORDERS[part][: stage + 1]:
-        sizes[axis] = None
-    if stage < 2:
-        sizes[ORDERS[part][stage + 1]] = 2
-        rows = r1 - r0
-    else:
-        rows = SPLITS[part][0]
-    return tuple(n for n in sizes if n is not None) + (rows, c1 - c0)
+    if stage == 2:
+        return (SPLITS[part][0], c1 - c0)
+    return ((8 if stage == 0 else 2) * (r1 - r0) + 16, c1 - c0)
+
+
+def half_type(stage):
+    return jnp.float32 if stage == 2 else jnp.int16
+
+
+LEVELS = 32767.0
 
 
 def scatter_kernel(slot_ref, parts_ref, grad_ref, acc, outbox, inbox, *rest):
-    buffers = rest[:9]
-    send, recv, pair_send, pair_recv = rest[9:]
+    landed = rest[:9]
+    packed = rest[9:15]
+    send, recv, pair_send, pair_recv = rest[15:]
     place = Place()
     edge = parts_ref.shape[1]
 
-    def region(ref, part, stage, k, half):
+    def spans(part, stage, k, half):
         order = ORDERS[part]
         (r0, r1), (c0, c1) = CUTS[part]
-        index = [slice(None)] * 3
+        index = [slice(0, RING)] * 3
         for axis in order[:stage]:
             index[axis] = 0
         index[order[stage]] = k
@@ -307,29 +315,73 @@
             else:
                 cut = r0 + SPLITS[part][0]
                 r0, r1 = (r0, cut) if half == 0 else (cut, r1)
-        return ref.at[index[0], index[1], index[2], r0:r1, c0:c1]
+        return index, slice(r0, r1), slice(c0, c1)
+
+    def region(ref, part, stage, k, half):
+        index, rows, cols = spans(part, stage, k, half)
+        return ref.at[index[0], index[1], index[2], rows, cols]
+
+    def cells(part, stage, k, half):
+        index, rows, cols = spans(part, stage, k, half)
+        each = [range(i.start, i.stop) if isinstance(i, slice) else (i,) for i in index]
+        return [acc.at[x, y, z, rows, cols] for x in each[0] for y in each[1] for z in each[2]]
 
     def half_of(way, k):
         return way if k != 1 else 1 - way
 
     def landing(part, stage, way, k):
-        ref = buffers[part * 3 + stage].at[way, k]
+        ref = landed[part * 3 + stage].at[way, k]
         if stage == 2:
             ref = ref.at[0 : SPLITS[part][half_of(way, k)]]
         return ref
 
-    def outgoing(part, stage, way, k):
-        offset = 2 if k == 0 else (3 if way == 0 else 1)
-        src = region(acc, part, stage, offset, half_of(way, k))
+    def source(part, stage, way, k):
+        if stage < 2:
+            return packed[part * 2 + stage].at[way, k]
+        return region(acc, part, stage, 2 if k == 0 else (3 if way == 0 else 1), half_of(way, k))
+
+    def transfer(part, stage, way, k):
         device = place.neighbour(ORDERS[part][stage], -1 if way == 0 else 1)
         at = (part, stage, way, k)
-        return remote(src, landing(part, stage, way, k), send.at[at], recv.at[at], device)
+        return remote(
+            source(part, stage, way, k), landing(part, stage, way, k), send.at[at], recv.at[at], device
+        )
+
+    def emit(part, stage, way, k):
+        if stage < 2:
+            refs = cells(part, stage, 2 if k == 0 else (3 if way == 0 else 1), half_of(way, k))
+            rows = refs[0].shape[0]
+            peak = jnp.abs(refs[0][...])
+            for ref in refs[1:]:
+                peak = jnp.maximum(peak, jnp.abs(ref[...]))
+            peak = jnp.maximum(jnp.max(peak, axis=0, keepdims=True), 1e-30)
+            power = jnp.ceil(jnp.log2(peak))
+            factor = jnp.exp2(-power) * LEVELS
+            out = source(part, stage, way, k)
+            for i in range(0, len(refs), 2):
+                both = jnp.concatenate([refs[i][...], refs[i + 1][...]], axis=0)
+                out[i * rows : (i + 2) * rows, :] = (
+                    jnp.round(both * factor).astype(jnp.int32).astype(jnp.int16)
+                )
+            out[len(refs) * rows :, :] = jnp.broadcast_to(
+                power, (16, power.shape[1])
+            ).astype(jnp.int32).astype(jnp.int16)
+        transfer(part, stage, way, k).start()
 
     def take(part, stage, way, k):
-        outgoing(part, stage, way, k).wait_recv()
-        offset = (3 if way == 0 else 1) if k == 0 else 0
-        target = region(acc, part, stage, offset, half_of(way, k))
-        target[...] = target[...] + landing(part, stage, way, k)[...]
+        transfer(part, stage, way, k).wait_recv()
+        refs = cells(part, stage, (3 if way == 0 else 1) if k == 0 else 0, half_of(way, k))
+        came = landing(part, stage, way, k)
+        if stage == 2:
+            refs[0][...] = refs[0][...] + came[...]
+            return
+        rows = refs[0].shape[0]
+        power = came[len(refs) * rows :, :].astype(jnp.int32).astype(jnp.float32)[:1]
+        factor = jnp.exp2(power) * (1.0 / LEVELS)
+        for i in range(0, len(refs), 2):
+            both = came[i * rows : (i + 2) * rows, :].astype(jnp.int32).astype(jnp.float32) * factor
+            refs[i][...] = refs[i][...] + both[:rows]
+            refs[i + 1][...] = refs[i + 1][...] + both[rows:]
 
     def across(part, k):
         at = (part, k)
@@ -359,8 +411,9 @@
                     slot_ref[first + j]
                 ]
 
+    place.announce()
     spread(outbox, 1 - place.core)
-    place.greet()
+    place.await_peers()
     for k in (2, 3, 1, 0):
         for part in range(3):
             across(part, k).start()
@@ -368,16 +421,16 @@
     for part in range(3):
         take_across(part, 2)
         for way in range(2):
-            outgoing(part, 0, way, 0).start()
+            emit(part, 0, way, 0)
     for part in range(3):
         for way, k in ((0, 3), (1, 1)):
             take_across(part, k)
-            outgoing(part, 0, way, 1).start()
+            emit(part, 0, way, 1)
     for stage in range(3):
         for part in range(3):
             for way in range(2):
                 take(part, stage, way, 0)
-                outgoing(part, stage, way, 2).start()
+                emit(part, stage, way, 2)
         if stage == 0:
             for part in range(3):
                 take_across(part, 0)
@@ -388,7 +441,7 @@
             if stage < 2:
                 for k in range(2):
                     for way in range(2):
-                        outgoing(part, stage + 1, way, k).start()
+                        emit(part, stage + 1, way, k)
     grad_ref[...] = acc[0, 0, 0]
     for part in range(3):
         for k in range(4):
@@ -396,16 +449,17 @@
         for stage in range(3):
             for way in range(2):
                 for k in range(3):
-                    outgoing(part, stage, way, k).wait_send()
+                    transfer(part, stage, way, k).wait_send()
 
 
 def scatter_gradients(parts, slot_of):
     edge, rank = parts.shape[1:]
     dense = (RING, RING, RING, 2 * edge, rank)
     buffers = [
-        pltpu.VMEM((2, 3) + half_shape(part, stage), jnp.float32)
+        pltpu.VMEM((2, 3) + half_shape(part, stage), half_type(stage))
+        for stages in (range(3), range(2))
         for part in range(3)
-        for stage in range(3)
+        for stage in stages
     ]
     return pl.pallas_call(
         scatter_kernel,

time: 166 us -> 153 us (0.922)
  Pallas kernels: 163 us -> 150 us
    pallas_call x1, Pallas kernels: 44 us -> 31.5 us  [block_gradients(): pl.pallas_call(functools.partial(block_kernel, local_blocks), out_shape=(...]
where the time goes in v5:
time: 153 us
  Pallas kernels  150 us (98%)
  other arithmetic  1.75 us (1%)
    pallas_call x1, Pallas kernels, gather_rows(): pl.pallas_call(gather_kernel, out_shape=jax.ShapeDtypeStruct((4, 4, 2, 4,...  66.4 us
    pallas_call x1, Pallas kernels, scatter_gradients(): pl.pallas_call(scatter_kernel, out_shape=jax.ShapeDtypeStruct((2 * edge,...  52.1 us
    pallas_call x1, Pallas kernels, block_gradients(): pl.pallas_call(functools.partial(block_kernel, local_blocks), out_shape=(...  31.5 us

profile of v5, /device:TPU:0, one launch (start us, length us, event | category | flops | bytes accessed | tf_op | source)
XLA Modules:
  0.0 153.0 jit_solution(12994199075179128903)
XLA Ops:
  1.3 66.4 %shard_map.94 = bf16[4,4,2,4,3,128,256]{6,5,4,3,2,1,0:T(8,128)(2,1)} custom-call(f32[3,128,256]{2,1,0:T(8,128)} %own_ref.1), custom_call_target="tpu_custom_call" | custom-call | tf_op jit(solution)/shard_map/pallas_call | solution.py:139
  67.7 0.0 copy-start
  67.7 0.0 copy-start.1
  67.7 31.5 %shard_map.95 = (f32[37,64,256]{2,1,0:T(8,128)}, s32[256]{0:T(256)}) custom-call(s32[3,36]{1,0:T(4,128)} %coords_ref.1, s32[3,256]{1,0:T(4,128)} %owner_ref.1, s32[1]{0:T(128)S(6)} %copy.10.count_ref, bf16[36,64,4096]{2,1,0:T(8,128)(2,1)} %blocks_ref.1, bf16[768,64,256]{2,1,0:T(8,128)(2,1)} %bitcast.3), custom_call_target="tpu_custom_call" | custom-call | flops 9663676416 | bytes 24772608 | tf_op jit(solution)/shard_map/pallas_call | solution.py:256
  99.2 52.1 %shard_map.96 = f32[128,256]{1,0:T(8,128)} custom-call(s32[256]{0:T(256)} %get-tuple-element.5.slot_ref, f32[37,64,256]{2,1,0:T(8,128)} %get-tuple-element.6.parts_ref), custom_call_target="tpu_custom_call" | custom-call | tf_op jit(solution)/shard_map/pallas_call | solution.py:464
  151.3 0.0 copy-done
  151.3 0.0 copy-done.1
  151.3 1.8 %bitcast_subtract_fusion = (f32[128,256]{1,0:T(8,128)}, f32[128,256]{1,0:T(8,128)}, f32[128,256]{1,0:T(8,128)}) fusion(f32[3,128,256]{2,1,0:T(8,128)} %own_ref.1, f32[128,256]{1,0:T(8,128)} %shard_map.96, f32[128,256]{1,0:T(8,128)S(1)} %copy-done, f32[128,256]{1,0:T(8,128)S(1)} %copy-done.1), kind=kLoop, calls=%fused_computation.2 | loop fusion | flops 393216 | bytes 917504 | tf_op jit(solution)/shard_map/sub | solution.py:498
Async XLA Ops:
  67.7 83.6 %copy-start = (f32[128,256]{1,0:T(8,128)S(1)}, f32[128,256]{1,0:T(8,128)}, u32[]{:S(2)}) copy-start(f32[128,256]{1,0:T(8,128)} %param.12) | copy-start | bytes 393220
  67.7 83.6 %copy-start.1 = (f32[128,256]{1,0:T(8,128)S(1)}, f32[128,256]{1,0:T(8,128)}, u32[]{:S(2)}) copy-start(f32[128,256]{1,0:T(8,128)} %param.13) | copy-start | bytes 393220

commit v6 on v5

--- a/solution.py
+++ b/solution.py
@@ -154,16 +154,37 @@
     )(factors)
 
 
-def block_part(edge, chunk, half_a, b_ref, rows_c, block_ref):
-    total = jnp.zeros((edge, rows_c.shape[1]), jnp.float32)
-    width = chunk * edge
-    for step in range(edge // chunk):
+GROUP = 4
+CHUNK = 16
+
+
+def block_part(rows_ref, block_ref):
+    _, edge, rank = rows_ref.shape
+    half_a = rows_ref[0] * jnp.bfloat16(0.5)
+    rows_c = rows_ref[2]
+    width = CHUNK * edge
+    twice = lambda rows: jnp.concatenate([rows, rows], axis=0).astype(jnp.float32).T
+    cols_b = twice(rows_ref[1])
+    cols_c = twice(rows_c).astype(jnp.bfloat16)
+    lane = lax.broadcasted_iota(jnp.int32, (rank, 2 * edge), 1)
+    total = jnp.zeros((edge, rank), jnp.float32)
+    for step in range(edge // CHUNK):
         pair = jnp.concatenate(
-            [b_ref[pl.ds(step * chunk + j, 1), :] * rows_c for j in range(chunk)], axis=0
+            [rows_ref[1, pl.ds(step * CHUNK + j, 1), :] * rows_c for j in range(CHUNK)], axis=0
         )
-        model = lax.dot_general(
-            half_a, pair, (((1,), (1,)), ((), ())), preferred_element_type=jnp.float32
-        )
+        if step == 0:
+            model = lax.dot_general(
+                half_a, pair, (((1,), (1,)), ((), ())), preferred_element_type=jnp.float32
+            )
+        else:
+            pieces = []
+            for j in range(step * CHUNK, (step + 1) * CHUNK, 2):
+                pick = jnp.where(lane < edge, j, j + 1)
+                spread = jnp.take_along_axis(cols_b, pick, axis=1).astype(jnp.bfloat16)
+                pieces.append(spread * cols_c)
+            model = jnp.dot(
+                half_a, jnp.concatenate(pieces, axis=1), preferred_element_type=jnp.float32
+            )
         observed = block_ref[:, step * width : (step + 1) * width].astype(jnp.float32)
         resid = (0.5 * jnp.tanh(model) + (0.5 - observed)).astype(jnp.bfloat16)
         total = total + jnp.dot(resid, pair, preferred_element_type=jnp.float32)
@@ -172,32 +193,50 @@
 
 def block_kernel(
     local_blocks, coords_ref, owner_ref, count_ref, blocks_ref, table_ref, parts_ref, slot_ref,
-    block_buf, rows_buf, part_buf, sems, part_sems,
+    block_buf, rows_buf, part_buf, row_of, block_sems, rows_sems, part_sems,
 ):
-    slots, edge, _ = blocks_ref.shape
-    depth = block_buf.shape[0]
-    modes = rows_buf.shape[1]
+    slots = blocks_ref.shape[0]
+    modes = rows_buf.shape[2]
     count = count_ref[0]
-
-    def copies(s):
-        at = lax.rem(s, depth)
-        made = [pltpu.make_async_copy(blocks_ref.at[s], block_buf.at[at], sems.at[at, modes])]
+    groups = lax.div(count + (GROUP - 1), GROUP)
+
+    def block_copy(h):
+        at = lax.rem(h, 2)
+        return pltpu.make_async_copy(
+            blocks_ref.at[pl.ds(h * GROUP, GROUP)], block_buf.at[at], block_sems.at[at]
+        )
+
+    def start_rows(h):
+        at = lax.rem(h, 2)
+        for q in range(GROUP):
+            for m in range(modes):
+                pltpu.make_async_copy(
+                    table_ref.at[row_of[m, h * GROUP + q]], rows_buf.at[at, q, m], rows_sems.at[at]
+                ).start()
+
+    def wait_rows(h):
+        at = lax.rem(h, 2)
+        pltpu.make_async_copy(rows_buf.at[at], rows_buf.at[at], rows_sems.at[at]).wait()
+
+    def store(h):
+        span = pl.ds(h * GROUP, GROUP)
+        return pltpu.make_async_copy(part_buf.at[span], parts_ref.at[span], part_sems.at[h])
+
+    last = pltpu.make_async_copy(
+        part_buf.at[slots], parts_ref.at[slots], part_sems.at[slots // GROUP]
+    )
+
+    block_copy(0).start()
+
+    @pl.loop(0, slots)
+    def _(s):
         for m in range(modes):
             pos = owner_ref[m, coords_ref[m, s]]
-            row = (lax.div(pos, local_blocks) * modes + m) * local_blocks + lax.rem(pos, local_blocks)
-            made.append(
-                pltpu.make_async_copy(table_ref.at[row], rows_buf.at[at, m], sems.at[at, m])
-            )
-        return made
-
-    def fetch(s):
-        @pl.when(s < count)
-        def _():
-            for copy in copies(s):
-                copy.start()
-
-    for s in range(depth - 2):
-        fetch(s)
+            row_of[m, s] = (
+                lax.div(pos, local_blocks) * modes + m
+            ) * local_blocks + lax.rem(pos, local_blocks)
+
+    start_rows(0)
 
     @pl.loop(0, slot_ref.shape[0])
     def _(p):
@@ -207,50 +246,35 @@
     def _(s):
         slot_ref[owner_ref[0, coords_ref[0, s]]] = s
 
-    def store(s):
-        return pltpu.make_async_copy(part_buf.at[s], parts_ref.at[s], part_sems.at[s])
-
     part_buf[slots] = jnp.zeros(part_buf.shape[1:], jnp.float32)
-    store(slots).start()
-
-    def compute(s):
-        at = lax.rem(s, depth)
-        half_a = rows_buf[at, 0] * jnp.bfloat16(0.5)
-        part_buf[s] = block_part(
-            edge, 16, half_a, rows_buf.at[at, 1], rows_buf[at, 2], block_buf.at[at]
-        )
-        store(s).start()
-
-    pairs = lax.div(count, 2)
-
-    @pl.loop(0, pairs)
+    last.start()
+
+    @pl.loop(0, groups)
     def _(h):
-        for q in range(2):
-            fetch(2 * h + depth - 2 + q)
-        for q in range(2):
-            for copy in copies(2 * h + q):
-                copy.wait()
-        for q in range(2):
-            compute(2 * h + q)
-
-    @pl.when(2 * pairs < count)
-    def _():
-        for copy in copies(2 * pairs):
-            copy.wait()
-        compute(2 * pairs)
-
-    @pl.loop(0, count)
-    def _(s):
-        store(s).wait()
-
-    store(slots).wait()
+        at = lax.rem(h, 2)
+
+        @pl.when(h + 1 < groups)
+        def _():
+            block_copy(h + 1).start()
+            start_rows(h + 1)
+
+        block_copy(h).wait()
+        wait_rows(h)
+        for q in range(GROUP):
+            part_buf[h * GROUP + q] = block_part(rows_buf.at[at, q], block_buf.at[at, q])
+        store(h).start()
+
+    @pl.loop(0, groups)
+    def _(h):
+        store(h).wait()
+
+    last.wait()
 
 
 def block_gradients(tensor_blocks, table, coords, owner, count, positions, local_blocks):
     slots, edge, merged = tensor_blocks.shape
     modes, _ = coords.shape
     rank = table.shape[2]
-    depth = 6
     smem = pl.BlockSpec(memory_space=pltpu.SMEM)
     far = pl.BlockSpec(memory_space=pltpu.HBM)
     return pl.pallas_call(
@@ -262,11 +286,13 @@
         in_specs=[smem, smem, smem, far, far],
         out_specs=(far, smem),
         scratch_shapes=[
-            pltpu.VMEM((depth, edge, merged), jnp.bfloat16),
-            pltpu.VMEM((depth, modes, edge, rank), jnp.bfloat16),
+            pltpu.VMEM((2, GROUP, edge, merged), jnp.bfloat16),
+            pltpu.VMEM((2, GROUP, modes, edge, rank), jnp.bfloat16),
             pltpu.VMEM((slots + 1, edge, rank), jnp.float32),
-            pltpu.SemaphoreType.DMA((depth, modes + 1)),
-            pltpu.SemaphoreType.DMA((slots + 1,)),
+            pltpu.SMEM((modes, slots), jnp.int32),
+            pltpu.SemaphoreType.DMA((2,)),
+            pltpu.SemaphoreType.DMA((2,)),
+            pltpu.SemaphoreType.DMA((slots // GROUP + 1,)),
         ],
         compiler_params=pltpu.CompilerParams(vmem_limit_bytes=62 << 20),
         cost_estimate=pl.CostEstimate(

time: 153 us -> 146 us (0.954)
  Pallas kernels: 150 us -> 143 us
    pallas_call x1, Pallas kernels: 52.1 us -> 43.1 us  [scatter_gradients(): pl.pallas_call(scatter_kernel, out_shape=jax.ShapeDtypeStruct((2 * edge,...]
    pallas_call x1, Pallas kernels: 31.5 us -> 33.5 us  [block_gradients(): pl.pallas_call(functools.partial(block_kernel, local_blocks), out_shape=(...]
where the time goes in v6:
time: 146 us
  Pallas kernels  143 us (98%)
  other arithmetic  1.75 us (1%)
    pallas_call x1, Pallas kernels, gather_rows(): pl.pallas_call(gather_kernel, out_shape=jax.ShapeDtypeStruct((4, 4, 2, 4,...  66.4 us
    pallas_call x1, Pallas kernels, scatter_gradients(): pl.pallas_call(scatter_kernel, out_shape=jax.ShapeDtypeStruct((2 * edge,...  43.1 us
    pallas_call x1, Pallas kernels, block_gradients(): pl.pallas_call(functools.partial(block_kernel, local_blocks), out_shape=(...  33.5 us

profile of v6, /device:TPU:0, one launch (start us, length us, event | category | flops | bytes accessed | tf_op | source)
XLA Modules:
  0.0 146.1 jit_solution(1890886068651977991)
XLA Ops:
  1.3 66.4 %shard_map.94 = bf16[4,4,2,4,3,128,256]{6,5,4,3,2,1,0:T(8,128)(2,1)} custom-call(f32[3,128,256]{2,1,0:T(8,128)} %own_ref.1), custom_call_target="tpu_custom_call" | custom-call | tf_op jit(solution)/shard_map/pallas_call | solution.py:139
  67.7 0.0 copy-start
  67.7 0.0 copy-start.1
  67.7 33.5 %shard_map.95 = (f32[37,64,256]{2,1,0:T(8,128)}, s32[256]{0:T(256)}) custom-call(s32[3,36]{1,0:T(4,128)} %coords_ref.1, s32[3,256]{1,0:T(4,128)} %owner_ref.1, s32[1]{0:T(128)S(6)} %copy.10.count_ref, bf16[36,64,4096]{2,1,0:T(8,128)(2,1)} %blocks_ref.1, bf16[768,64,256]{2,1,0:T(8,128)(2,1)} %bitcast.3), custom_call_target="tpu_custom_call" | custom-call | flops 9663676416 | bytes 24772608 | tf_op jit(solution)/shard_map/pallas_call | solution.py:280
  101.2 43.1 %shard_map.96 = f32[128,256]{1,0:T(8,128)} custom-call(s32[256]{0:T(256)} %get-tuple-element.5.slot_ref, f32[37,64,256]{2,1,0:T(8,128)} %get-tuple-element.6.parts_ref), custom_call_target="tpu_custom_call" | custom-call | tf_op jit(solution)/shard_map/pallas_call | solution.py:490
  144.3 0.0 copy-done
  144.4 0.0 copy-done.1
  144.4 1.8 %bitcast_subtract_fusion = (f32[128,256]{1,0:T(8,128)}, f32[128,256]{1,0:T(8,128)}, f32[128,256]{1,0:T(8,128)}) fusion(f32[3,128,256]{2,1,0:T(8,128)} %own_ref.1, f32[128,256]{1,0:T(8,128)} %shard_map.96, f32[128,256]{1,0:T(8,128)S(1)} %copy-done, f32[128,256]{1,0:T(8,128)S(1)} %copy-done.1), kind=kLoop, calls=%fused_computation.2 | loop fusion | flops 393216 | bytes 917504 | tf_op jit(solution)/shard_map/sub | solution.py:524
Async XLA Ops:
  67.7 76.7 %copy-start = (f32[128,256]{1,0:T(8,128)S(1)}, f32[128,256]{1,0:T(8,128)}, u32[]{:S(2)}) copy-start(f32[128,256]{1,0:T(8,128)} %param.12) | copy-start | bytes 393220
  67.7 76.7 %copy-start.1 = (f32[128,256]{1,0:T(8,128)S(1)}, f32[128,256]{1,0:T(8,128)}, u32[]{:S(2)}) copy-start(f32[128,256]{1,0:T(8,128)} %param.13) | copy-start | bytes 393220

commit v7 on v6

--- a/solution.py
+++ b/solution.py
@@ -61,20 +61,30 @@
     other = 1 - core
     half_rows = cast_ref.shape[1] // 2
 
-    def region(part, stage, value, half, side):
+    def region(part, stage, value, half, side, piece=None):
+        order = ORDERS[part]
         index = list(place.coord)
-        for axis in ORDERS[part][:stage]:
+        for axis in order[:stage]:
             index[axis] = slice(None)
-        index[ORDERS[part][stage]] = value
+        if piece is not None:
+            index[order[stage - 1]] = piece
+        index[order[stage]] = value
         return table_ref.at[
             index[0], index[1], side, index[2], part, half * half_rows : (half + 1) * half_rows
         ]
+
+    def passed(stage):
+        return range(2, 3) if stage < 2 else range(2, 2 + RING)
+
+    def piece_of(stage, k):
+        return k - 2 if stage == 2 and k >= 2 else None
 
     def arrived(part, stage, way, k, side):
         axis = ORDERS[part][stage]
         step = -1 if way == 0 else 1
         value = place.along(axis, step if k < 2 else 2)
-        return region(part, stage, value, way if k != 1 else 1 - way, side)
+        half = way if k != 1 else 1 - way
+        return region(part, stage, value, half, side, piece_of(stage, k))
 
     def outgoing(part, stage, way, k):
         axis = ORDERS[part][stage]
@@ -85,7 +95,8 @@
             if stage == 0:
                 src = cast_ref.at[part, half * half_rows : (half + 1) * half_rows]
         else:
-            dst = src = arrived(part, stage, way, 0, core)
+            value = place.along(axis, -1 if way == 0 else 1)
+            dst = src = region(part, stage, value, half, core, piece_of(stage, k))
         device = place.neighbour(axis, 1 if way == 0 else -1)
         return remote(src, dst, send.at[part, stage, way, k], recv.at[part, stage, way, k], device)
 
@@ -100,8 +111,16 @@
         at = (part, stage, way, k)
         return remote(ref, ref, pair_send.at[at], pair_recv.at[at], place.partner())
 
+    def drain(stage, ks):
+        for k in ks:
+            for part, way in steps:
+                outgoing(part, stage, way, k).wait_send()
+                across(part, stage, way, k, core).wait_send()
+                across(part, stage, way, k, other).wait_recv()
+
+    place.announce()
     cast_ref[...] = own_ref[...].astype(cast_ref.dtype)
-    place.greet()
+    place.await_peers()
     steps = [(part, way) for part in range(3) for way in range(2)]
     for k in range(2):
         for part, way in steps:
@@ -112,26 +131,27 @@
     own.start()
     mine.wait()
     for stage in range(3):
-        for k in range(3):
+        for k in (0, 1) + tuple(passed(stage)):
+            if stage == 2 and k == 1:
+                own.wait_send()
+                theirs = table_ref.at[x, y, other, z]
+                remote(theirs, theirs, own_sem.at[0], own_sem.at[1], place.partner()).wait_recv()
+                for before in range(2):
+                    drain(before, (0, 1) + tuple(passed(before)))
+            if stage == 2 and k == 2:
+                drain(2, (0,))
             for part in range(3):
                 for way in range(2):
                     incoming(part, stage, way, k).wait_recv()
                     if k == 0:
-                        outgoing(part, stage, way, 2).start()
+                        for later in passed(stage):
+                            outgoing(part, stage, way, later).start()
                     across(part, stage, way, k, core).start()
                 if k == 2 and stage < 2:
                     for way in range(2):
                         outgoing(part, stage + 1, way, 0).start()
                         outgoing(part, stage + 1, way, 1).start()
-    own.wait_send()
-    theirs = table_ref.at[x, y, other, z]
-    remote(theirs, theirs, own_sem.at[0], own_sem.at[1], place.partner()).wait_recv()
-    for stage in range(3):
-        for k in range(3):
-            for part, way in steps:
-                outgoing(part, stage, way, k).wait_send()
-                across(part, stage, way, k, core).wait_send()
-                across(part, stage, way, k, other).wait_recv()
+    drain(2, (1,) + tuple(passed(2)))
 
 
 def gather_rows(factors):
@@ -145,10 +165,10 @@
             pltpu.VMEM((modes, rows, rank), jnp.bfloat16),
             pltpu.SemaphoreType.DMA,
             pltpu.SemaphoreType.DMA((2,)),
-            pltpu.SemaphoreType.DMA((3, 3, 2, 3)),
-            pltpu.SemaphoreType.DMA((3, 3, 2, 3)),
-            pltpu.SemaphoreType.DMA((3, 3, 2, 3)),
-            pltpu.SemaphoreType.DMA((3, 3, 2, 3)),
+            pltpu.SemaphoreType.DMA((3, 3, 2, 2 + RING)),
+            pltpu.SemaphoreType.DMA((3, 3, 2, 2 + RING)),
+            pltpu.SemaphoreType.DMA((3, 3, 2, 2 + RING)),
+            pltpu.SemaphoreType.DMA((3, 3, 2, 2 + RING)),
         ],
         compiler_params=pltpu.CompilerParams(collective_id=0, has_side_effects=True),
     )(factors)
@@ -228,15 +248,20 @@
 
     block_copy(0).start()
 
-    @pl.loop(0, slots)
-    def _(s):
+    def look_up(s):
         for m in range(modes):
             pos = owner_ref[m, coords_ref[m, s]]
             row_of[m, s] = (
                 lax.div(pos, local_blocks) * modes + m
             ) * local_blocks + lax.rem(pos, local_blocks)
 
+    for s in range(GROUP):
+        look_up(s)
     start_rows(0)
+
+    @pl.loop(GROUP, slots)
+    def _(s):
+        look_up(s)
 
     @pl.loop(0, slot_ref.shape[0])
     def _(p):
@@ -437,6 +462,11 @@
                     slot_ref[first + j]
                 ]
 
+    def sent(part, stage):
+        for way in range(2):
+            for k in range(3):
+                transfer(part, stage, way, k).wait_send()
+
     place.announce()
     spread(outbox, 1 - place.core)
     place.await_peers()
@@ -460,6 +490,12 @@
         if stage == 0:
             for part in range(3):
                 take_across(part, 0)
+        if stage == 2:
+            for part in range(3):
+                for k in range(4):
+                    across(part, k).wait_send()
+                for before in range(2):
+                    sent(part, before)
         for part in range(3):
             for k in (1, 2):
                 for way in range(2):
@@ -470,12 +506,7 @@
                         emit(part, stage + 1, way, k)
     grad_ref[...] = acc[0, 0, 0]
     for part in range(3):
-        for k in range(4):
-            across(part, k).wait_send()
-        for stage in range(3):
-            for way in range(2):
-                for k in range(3):
-                    transfer(part, stage, way, k).wait_send()
+        sent(part, 2)
 
 
 def scatter_gradients(parts, slot_of):

time: 146 us -> 145 us (level)
    pallas_call x1, Pallas kernels: 33.5 us -> 15.5 us  [block_gradients(): pl.pallas_call(functools.partial(block_kernel, local_blocks), out_shape=(...]
    pallas_call x1, Pallas kernels: 43.1 us -> 60.6 us  [scatter_gradients(): pl.pallas_call(scatter_kernel, out_shape=jax.ShapeDtypeStruct((2 * edge,...]
where the time goes in v7:
time: 145 us
  Pallas kernels  142 us (98%)
  other arithmetic  1.75 us (1%)
    pallas_call x1, Pallas kernels, gather_rows(): pl.pallas_call(gather_kernel, out_shape=jax.ShapeDtypeStruct((4, 4, 2, 4,...  65.5 us
    pallas_call x1, Pallas kernels, scatter_gradients(): pl.pallas_call(scatter_kernel, out_shape=jax.ShapeDtypeStruct((2 * edge,...  60.6 us
    pallas_call x1, Pallas kernels, block_gradients(): pl.pallas_call(functools.partial(block_kernel, local_blocks), out_shape=(...  15.5 us

profile of v7, /device:TPU:0, one launch (start us, length us, event | category | flops | bytes accessed | tf_op | source)
XLA Modules:
  0.0 144.8 jit_solution(14206584373224819107)
XLA Ops:
  1.3 65.5 %shard_map.94 = bf16[4,4,2,4,3,128,256]{6,5,4,3,2,1,0:T(8,128)(2,1)} custom-call(f32[3,128,256]{2,1,0:T(8,128)} %own_ref.1), custom_call_target="tpu_custom_call" | custom-call | tf_op jit(solution)/shard_map/pallas_call | solution.py:159
  66.8 0.0 copy-start
  66.8 0.0 copy-start.1
  66.9 15.5 %shard_map.95 = (f32[37,64,256]{2,1,0:T(8,128)}, s32[256]{0:T(256)}) custom-call(s32[3,36]{1,0:T(4,128)} %coords_ref.1, s32[3,256]{1,0:T(4,128)} %owner_ref.1, s32[1]{0:T(128)S(6)} %copy.10.count_ref, bf16[36,64,4096]{2,1,0:T(8,128)(2,1)} %blocks_ref.1, bf16[768,64,256]{2,1,0:T(8,128)(2,1)} %bitcast.3), custom_call_target="tpu_custom_call" | custom-call | flops 9663676416 | bytes 24772608 | tf_op jit(solution)/shard_map/pallas_call | solution.py:305
  82.4 60.6 %shard_map.96 = f32[128,256]{1,0:T(8,128)} custom-call(s32[256]{0:T(256)} %get-tuple-element.5.slot_ref, f32[37,64,256]{2,1,0:T(8,128)} %get-tuple-element.6.parts_ref), custom_call_target="tpu_custom_call" | custom-call | tf_op jit(solution)/shard_map/pallas_call | solution.py:521
  143.0 0.0 copy-done
  143.0 0.0 copy-done.1
  143.0 1.8 %bitcast_subtract_fusion = (f32[128,256]{1,0:T(8,128)}, f32[128,256]{1,0:T(8,128)}, f32[128,256]{1,0:T(8,128)}) fusion(f32[3,128,256]{2,1,0:T(8,128)} %own_ref.1, f32[128,256]{1,0:T(8,128)} %shard_map.96, f32[128,256]{1,0:T(8,128)S(1)} %copy-done, f32[128,256]{1,0:T(8,128)S(1)} %copy-done.1), kind=kLoop, calls=%fused_computation.2 | loop fusion | flops 393216 | bytes 917504 | tf_op jit(solution)/shard_map/sub | solution.py:555
Async XLA Ops:
  66.8 76.2 %copy-start = (f32[128,256]{1,0:T(8,128)S(1)}, f32[128,256]{1,0:T(8,128)}, u32[]{:S(2)}) copy-start(f32[128,256]{1,0:T(8,128)} %param.12) | copy-start | bytes 393220
  66.8 76.2 %copy-start.1 = (f32[128,256]{1,0:T(8,128)S(1)}, f32[128,256]{1,0:T(8,128)}, u32[]{:S(2)}) copy-start(f32[128,256]{1,0:T(8,128)} %param.13) | copy-start | bytes 393220

commit v8 on v7

--- a/solution.py
+++ b/solution.py
@@ -34,9 +34,12 @@
         coord[axis] = self.along(axis, step)
         return self.device(coord, self.core)
 
-    def greet(self):
-        self.announce()
-        self.await_peers()
+    def offset(self, device):
+        blk = lax.div(device, RING)
+        coord = (lax.div(blk, 8), lax.rem(lax.div(blk, 2), 4), lax.rem(device, RING))
+        steps = [lax.rem(v - me + RING, RING) for v, me in zip(coord, self.coord)]
+        side = lax.rem(lax.rem(blk, 2) + self.core, 2)
+        return ((steps[0] * RING + steps[1]) * RING + steps[2]) * 2 + side
 
     def announce(self):
         barrier = pltpu.get_barrier_semaphore()
@@ -54,127 +57,152 @@
     )
 
 
+ALL = slice(0, RING)
+FAR = slice(1, RING)
+GROUPS = (
+    ((),),
+    ((0,), (FAR,)),
+    ((0, 0), (FAR, 0), (ALL, 1), (ALL, 3), (ALL, 2)),
+)
+LISTED = [(stage, g) for stage in range(3) for g in range(len(GROUPS[stage]))]
+NUMBER = {at: i for i, at in enumerate(LISTED)}
+
+
 def gather_kernel(own_ref, table_ref, cast_ref, local_sem, own_sem, send, recv, pair_send, pair_recv):
     place = Place()
-    x, y, z = place.coord
-    core = place.core
-    other = 1 - core
     half_rows = cast_ref.shape[1] // 2
 
-    def region(part, stage, value, half, side, piece=None):
-        order = ORDERS[part]
-        index = list(place.coord)
-        for axis in order[:stage]:
-            index[axis] = slice(None)
-        if piece is not None:
-            index[order[stage - 1]] = piece
-        index[order[stage]] = value
-        return table_ref.at[
-            index[0], index[1], side, index[2], part, half * half_rows : (half + 1) * half_rows
-        ]
-
-    def passed(stage):
-        return range(2, 3) if stage < 2 else range(2, 2 + RING)
-
-    def piece_of(stage, k):
-        return k - 2 if stage == 2 and k >= 2 else None
-
-    def arrived(part, stage, way, k, side):
-        axis = ORDERS[part][stage]
-        step = -1 if way == 0 else 1
-        value = place.along(axis, step if k < 2 else 2)
-        half = way if k != 1 else 1 - way
-        return region(part, stage, value, half, side, piece_of(stage, k))
-
-    def outgoing(part, stage, way, k):
-        axis = ORDERS[part][stage]
-        half = way if k != 1 else 1 - way
-        if k < 2:
-            dst = region(part, stage, place.coord[axis], half, core)
-            src = dst
-            if stage == 0:
+    def region(part, stage, g, value, half, side):
+        index = [0, 0, 0]
+        for axis, piece in zip(ORDERS[part], GROUPS[stage][g]):
+            index[axis] = piece
+        index[ORDERS[part][stage]] = value
+        rows = slice(0, 2 * half_rows) if half is None else slice(half * half_rows, (half + 1) * half_rows)
+        return table_ref.at[index[0], index[1], index[2], side, part, rows]
+
+    def half_of(way, k):
+        return way if k != 1 else 1 - way
+
+    def copy(part, stage, g, way, k):
+        half = half_of(way, k)
+        came = 3 if way == 0 else 1
+        if k == 2:
+            src = region(part, stage, g, came, half, 0)
+            dst = region(part, stage, g, 2, half, 0)
+        else:
+            src = region(part, stage, g, 0, half, 0)
+            dst = region(part, stage, g, came, half, 0)
+            if g == 0:
                 src = cast_ref.at[part, half * half_rows : (half + 1) * half_rows]
-        else:
-            value = place.along(axis, -1 if way == 0 else 1)
-            dst = src = region(part, stage, value, half, core, piece_of(stage, k))
-        device = place.neighbour(axis, 1 if way == 0 else -1)
-        return remote(src, dst, send.at[part, stage, way, k], recv.at[part, stage, way, k], device)
-
-    def incoming(part, stage, way, k):
-        ref = arrived(part, stage, way, k, core)
-        axis = ORDERS[part][stage]
-        device = place.neighbour(axis, 1 if way == 0 else -1)
-        return remote(ref, ref, send.at[part, stage, way, k], recv.at[part, stage, way, k], device)
-
-    def across(part, stage, way, k, side):
-        ref = arrived(part, stage, way, k, side)
-        at = (part, stage, way, k)
-        return remote(ref, ref, pair_send.at[at], pair_recv.at[at], place.partner())
-
-    def drain(stage, ks):
-        for k in ks:
+        device = place.neighbour(ORDERS[part][stage], 1 if way == 0 else -1)
+        at = (part, NUMBER[stage, g], way, k)
+        return remote(src, dst, send.at[at], recv.at[at], device)
+
+    def across(part, stage, g, way, j):
+        value, half = ((3 if way == 0 else 1), None) if j == 0 else (2, way)
+        at = (part, NUMBER[stage, g], way, j)
+        return remote(
+            region(part, stage, g, value, half, 0),
+            region(part, stage, g, value, half, 1),
+            pair_send.at[at],
+            pair_recv.at[at],
+            place.partner(),
+        )
+
+    steps = [(part, way) for part in range(3) for way in range(2)]
+
+    def begin(stage, g):
+        for k in range(2):
             for part, way in steps:
-                outgoing(part, stage, way, k).wait_send()
-                across(part, stage, way, k, core).wait_send()
-                across(part, stage, way, k, other).wait_recv()
+                copy(part, stage, g, way, k).start()
+
+    def arrive(stage, g, k):
+        for part, way in steps:
+            copy(part, stage, g, way, k).wait_recv()
+            if k == 0:
+                copy(part, stage, g, way, 2).start()
+            else:
+                across(part, stage, g, way, k - 1).start()
+
+    def drain(stage, g):
+        for part, way in steps:
+            for k in range(3):
+                copy(part, stage, g, way, k).wait_send()
+            for j in range(2):
+                across(part, stage, g, way, j).wait_send()
+
+    def collect(stage, g):
+        for part, way in steps:
+            for j in range(2):
+                across(part, stage, g, way, j).wait_recv()
 
     place.announce()
     cast_ref[...] = own_ref[...].astype(cast_ref.dtype)
     place.await_peers()
-    steps = [(part, way) for part in range(3) for way in range(2)]
-    for k in range(2):
-        for part, way in steps:
-            outgoing(part, 0, way, k).start()
-    mine = pltpu.make_async_copy(cast_ref, table_ref.at[x, y, core, z], local_sem)
+    for stage in range(3):
+        begin(stage, 0)
+    mine = pltpu.make_async_copy(cast_ref, table_ref.at[0, 0, 0, 0], local_sem)
     mine.start()
-    own = remote(cast_ref, table_ref.at[x, y, core, z], own_sem.at[0], own_sem.at[1], place.partner())
+    own = remote(cast_ref, table_ref.at[0, 0, 0, 1], own_sem.at[0], own_sem.at[1], place.partner())
     own.start()
     mine.wait()
-    for stage in range(3):
-        for k in (0, 1) + tuple(passed(stage)):
-            if stage == 2 and k == 1:
-                own.wait_send()
-                theirs = table_ref.at[x, y, other, z]
-                remote(theirs, theirs, own_sem.at[0], own_sem.at[1], place.partner()).wait_recv()
-                for before in range(2):
-                    drain(before, (0, 1) + tuple(passed(before)))
-            if stage == 2 and k == 2:
-                drain(2, (0,))
-            for part in range(3):
-                for way in range(2):
-                    incoming(part, stage, way, k).wait_recv()
-                    if k == 0:
-                        for later in passed(stage):
-                            outgoing(part, stage, way, later).start()
-                    across(part, stage, way, k, core).start()
-                if k == 2 and stage < 2:
-                    for way in range(2):
-                        outgoing(part, stage + 1, way, 0).start()
-                        outgoing(part, stage + 1, way, 1).start()
-    drain(2, (1,) + tuple(passed(2)))
+    arrive(0, 0, 0)
+    arrive(0, 0, 1)
+    arrive(1, 0, 0)
+    arrive(0, 0, 2)
+    begin(1, 1)
+    begin(2, 1)
+    arrive(2, 0, 0)
+    for k in range(1, 3):
+        arrive(1, 0, k)
+        arrive(2, 0, k)
+    arrive(1, 1, 0)
+    arrive(1, 1, 1)
+    begin(2, 2)
+    begin(2, 3)
+    arrive(2, 1, 0)
+    arrive(1, 1, 2)
+    begin(2, 4)
+    arrive(2, 1, 1)
+    arrive(2, 1, 2)
+    own.wait()
+    for at in ((0, 0), (1, 0), (2, 0), (1, 1)):
+        drain(*at)
+        collect(*at)
+    for g in (2, 3, 4):
+        arrive(2, g, 0)
+        arrive(2, g, 1)
+    drain(2, 1)
+    collect(2, 1)
+    for g in (2, 3, 4):
+        arrive(2, g, 2)
+    for g in (2, 3, 4):
+        drain(2, g)
+        collect(2, g)
 
 
 def gather_rows(factors):
     modes, rows, rank = factors.shape
+    count = len(LISTED)
     return pl.pallas_call(
         gather_kernel,
-        out_shape=jax.ShapeDtypeStruct((4, 4, 2, 4, modes, rows, rank), jnp.bfloat16),
+        out_shape=jax.ShapeDtypeStruct((RING, RING, RING, 2, modes, rows, rank), jnp.bfloat16),
         in_specs=[pl.BlockSpec(memory_space=pltpu.VMEM)],
         out_specs=pl.BlockSpec(memory_space=pl.ANY),
         scratch_shapes=[
             pltpu.VMEM((modes, rows, rank), jnp.bfloat16),
             pltpu.SemaphoreType.DMA,
             pltpu.SemaphoreType.DMA((2,)),
-            pltpu.SemaphoreType.DMA((3, 3, 2, 2 + RING)),
-            pltpu.SemaphoreType.DMA((3, 3, 2, 2 + RING)),
-            pltpu.SemaphoreType.DMA((3, 3, 2, 2 + RING)),
-            pltpu.SemaphoreType.DMA((3, 3, 2, 2 + RING)),
+            pltpu.SemaphoreType.DMA((3, count, 2, 3)),
+            pltpu.SemaphoreType.DMA((3, count, 2, 3)),
+            pltpu.SemaphoreType.DMA((3, count, 2, 2)),
+            pltpu.SemaphoreType.DMA((3, count, 2, 2)),
         ],
         compiler_params=pltpu.CompilerParams(collective_id=0, has_side_effects=True),
     )(factors)
 
 
-GROUP = 4
+GROUP = 6
 CHUNK = 16
 
 
@@ -218,6 +246,7 @@
     slots = blocks_ref.shape[0]
     modes = rows_buf.shape[2]
     count = count_ref[0]
+    place = Place()
     groups = lax.div(count + (GROUP - 1), GROUP)
 
     def block_copy(h):
@@ -251,9 +280,8 @@
     def look_up(s):
         for m in range(modes):
             pos = owner_ref[m, coords_ref[m, s]]
-            row_of[m, s] = (
-                lax.div(pos, local_blocks) * modes + m
-            ) * local_blocks + lax.rem(pos, local_blocks)
+            row = (place.offset(lax.div(pos, local_blocks)) * modes + m) * local_blocks
+            row_of[m, s] = row + lax.rem(pos, local_blocks)
 
     for s in range(GROUP):
         look_up(s)

time: 145 us -> 144 us (level)
  Pallas kernels: 142 us -> 140 us
    pallas_call x1, Pallas kernels: 15.5 us -> 22.1 us  [block_gradients(): pl.pallas_call(functools.partial(block_kernel, local_blocks), out_shape=(...]
    pallas_call x1, Pallas kernels: 60.6 us -> 56 us  [scatter_gradients(): pl.pallas_call(scatter_kernel, out_shape=jax.ShapeDtypeStruct((2 * edge,...]
    pallas_call x1, Pallas kernels: 65.5 us -> 62.1 us  [gather_rows(): pl.pallas_call(gather_kernel, out_shape=jax.ShapeDtypeStruct((RING, RING,...]
where the time goes in v8:
time: 144 us; the launch traced here: 143 us
  Pallas kernels  140 us (97%)
  other arithmetic  1.75 us (1%)
    pallas_call x1, Pallas kernels, gather_rows(): pl.pallas_call(gather_kernel, out_shape=jax.ShapeDtypeStruct((RING, RING,...  62.1 us
    pallas_call x1, Pallas kernels, scatter_gradients(): pl.pallas_call(scatter_kernel, out_shape=jax.ShapeDtypeStruct((2 * edge,...  56 us
    pallas_call x1, Pallas kernels, block_gradients(): pl.pallas_call(functools.partial(block_kernel, local_blocks), out_shape=(...  22.1 us

profile of v8, /device:TPU:0, one launch (start us, length us, event | category | flops | bytes accessed | tf_op | source)
XLA Modules:
  0.0 143.3 jit_solution(12053733658524630302)
XLA Ops:
  1.3 62.1 %shard_map.94 = bf16[4,4,4,2,3,128,256]{6,5,4,3,2,1,0:T(8,128)(2,1)} custom-call(f32[3,128,256]{2,1,0:T(8,128)} %own_ref.1), custom_call_target="tpu_custom_call" | custom-call | tf_op jit(solution)/shard_map/pallas_call | solution.py:187
  63.4 0.0 copy-start
  63.4 0.0 copy-start.1
  63.4 22.1 %shard_map.95 = (f32[37,64,256]{2,1,0:T(8,128)}, s32[256]{0:T(256)}) custom-call(s32[3,36]{1,0:T(4,128)} %coords_ref.1, s32[3,256]{1,0:T(4,128)} %owner_ref.1, s32[1]{0:T(128)S(6)} %copy.10.count_ref, bf16[36,64,4096]{2,1,0:T(8,128)(2,1)} %blocks_ref.1, bf16[768,64,256]{2,1,0:T(8,128)(2,1)} %bitcast.3), custom_call_target="tpu_custom_call" | custom-call | flops 9663676416 | bytes 24772608 | tf_op jit(solution)/shard_map/pallas_call | solution.py:333
  85.5 56.0 %shard_map.96 = f32[128,256]{1,0:T(8,128)} custom-call(s32[256]{0:T(256)} %get-tuple-element.5.slot_ref, f32[37,64,256]{2,1,0:T(8,128)} %get-tuple-element.6.parts_ref), custom_call_target="tpu_custom_call" | custom-call | tf_op jit(solution)/shard_map/pallas_call | solution.py:549
  141.5 0.0 copy-done
  141.5 0.0 copy-done.1
  141.5 1.8 %bitcast_subtract_fusion = (f32[128,256]{1,0:T(8,128)}, f32[128,256]{1,0:T(8,128)}, f32[128,256]{1,0:T(8,128)}) fusion(f32[3,128,256]{2,1,0:T(8,128)} %own_ref.1, f32[128,256]{1,0:T(8,128)} %shard_map.96, f32[128,256]{1,0:T(8,128)S(1)} %copy-done, f32[128,256]{1,0:T(8,128)S(1)} %copy-done.1), kind=kLoop, calls=%fused_computation.2 | loop fusion | flops 393216 | bytes 917504 | tf_op jit(solution)/shard_map/sub | solution.py:583
Async XLA Ops:
  63.4 78.1 %copy-start = (f32[128,256]{1,0:T(8,128)S(1)}, f32[128,256]{1,0:T(8,128)}, u32[]{:S(2)}) copy-start(f32[128,256]{1,0:T(8,128)} %param.12) | copy-start | bytes 393220
  63.4 78.1 %copy-start.1 = (f32[128,256]{1,0:T(8,128)S(1)}, f32[128,256]{1,0:T(8,128)}, u32[]{:S(2)}) copy-start(f32[128,256]{1,0:T(8,128)} %param.13) | copy-start | bytes 393220

commit v9 on v8

--- a/solution.py
+++ b/solution.py
@@ -35,11 +35,11 @@
         return self.device(coord, self.core)
 
     def offset(self, device):
-        blk = lax.div(device, RING)
-        coord = (lax.div(blk, 8), lax.rem(lax.div(blk, 2), 4), lax.rem(device, RING))
-        steps = [lax.rem(v - me + RING, RING) for v, me in zip(coord, self.coord)]
-        side = lax.rem(lax.rem(blk, 2) + self.core, 2)
-        return ((steps[0] * RING + steps[1]) * RING + steps[2]) * 2 + side
+        blk = device >> 2
+        coord = (blk >> 3, (blk >> 1) & 3, device & 3)
+        steps = [(v - me) & 3 for v, me in zip(coord, self.coord)]
+        side = (blk ^ self.core) & 1
+        return (steps[0] << 5) | (steps[1] << 3) | (steps[2] << 1) | side
 
     def announce(self):
         barrier = pltpu.get_barrier_semaphore()
@@ -241,7 +241,7 @@
 
 def block_kernel(
     local_blocks, coords_ref, owner_ref, count_ref, blocks_ref, table_ref, parts_ref, slot_ref,
-    block_buf, rows_buf, part_buf, row_of, block_sems, rows_sems, part_sems,
+    block_buf, rows_buf, part_buf, block_sems, rows_sems, part_sems,
 ):
     slots = blocks_ref.shape[0]
     modes = rows_buf.shape[2]
@@ -249,22 +249,20 @@
     place = Place()
     groups = lax.div(count + (GROUP - 1), GROUP)
 
-    def block_copy(h):
-        at = lax.rem(h, 2)
+    def block_copy(h, at):
         return pltpu.make_async_copy(
             blocks_ref.at[pl.ds(h * GROUP, GROUP)], block_buf.at[at], block_sems.at[at]
         )
 
-    def start_rows(h):
-        at = lax.rem(h, 2)
-        for q in range(GROUP):
-            for m in range(modes):
-                pltpu.make_async_copy(
-                    table_ref.at[row_of[m, h * GROUP + q]], rows_buf.at[at, q, m], rows_sems.at[at]
-                ).start()
-
-    def wait_rows(h):
-        at = lax.rem(h, 2)
+    def start_rows(h, at, q):
+        for m in range(modes):
+            pos = owner_ref[m, coords_ref[m, h * GROUP + q]]
+            row = (place.offset(pos >> 1) * modes + m) * local_blocks + (pos & 1)
+            pltpu.make_async_copy(
+                table_ref.at[row], rows_buf.at[at, q, m], rows_sems.at[at]
+            ).start()
+
+    def wait_rows(at):
         pltpu.make_async_copy(rows_buf.at[at], rows_buf.at[at], rows_sems.at[at]).wait()
 
     def store(h):
@@ -275,21 +273,10 @@
         part_buf.at[slots], parts_ref.at[slots], part_sems.at[slots // GROUP]
     )
 
-    block_copy(0).start()
-
-    def look_up(s):
-        for m in range(modes):
-            pos = owner_ref[m, coords_ref[m, s]]
-            row = (place.offset(lax.div(pos, local_blocks)) * modes + m) * local_blocks
-            row_of[m, s] = row + lax.rem(pos, local_blocks)
-
-    for s in range(GROUP):
-        look_up(s)
-    start_rows(0)
-
-    @pl.loop(GROUP, slots)
-    def _(s):
-        look_up(s)
+    block_copy(0, 0).start()
+
+    for q in range(GROUP):
+        start_rows(0, 0, q)
 
     @pl.loop(0, slot_ref.shape[0])
     def _(p):
@@ -305,15 +292,12 @@
     @pl.loop(0, groups)
     def _(h):
         at = lax.rem(h, 2)
-
-        @pl.when(h + 1 < groups)
-        def _():
-            block_copy(h + 1).start()
-            start_rows(h + 1)
-
-        block_copy(h).wait()
-        wait_rows(h)
+        ahead = jnp.minimum(h + 1, groups - 1)
+        block_copy(h, at).wait()
+        wait_rows(at)
+        block_copy(ahead, 1 - at).start()
         for q in range(GROUP):
+            start_rows(ahead, 1 - at, q)
             part_buf[h * GROUP + q] = block_part(rows_buf.at[at, q], block_buf.at[at, q])
         store(h).start()
 
@@ -322,6 +306,8 @@
         store(h).wait()
 
     last.wait()
+    block_copy(0, lax.rem(groups, 2)).wait()
+    wait_rows(lax.rem(groups, 2))
 
 
 def block_gradients(tensor_blocks, table, coords, owner, count, positions, local_blocks):
@@ -342,7 +328,6 @@
             pltpu.VMEM((2, GROUP, edge, merged), jnp.bfloat16),
             pltpu.VMEM((2, GROUP, modes, edge, rank), jnp.bfloat16),
             pltpu.VMEM((slots + 1, edge, rank), jnp.float32),
-            pltpu.SMEM((modes, slots), jnp.int32),
             pltpu.SemaphoreType.DMA((2,)),
             pltpu.SemaphoreType.DMA((2,)),
             pltpu.SemaphoreType.DMA((slots // GROUP + 1,)),

time: 144 us -> 141 us (0.979)
  Pallas kernels: 140 us -> 138 us
    pallas_call x1, Pallas kernels: 56 us -> 51 us  [scatter_gradients(): pl.pallas_call(scatter_kernel, out_shape=jax.ShapeDtypeStruct((2 * edge,...]
    pallas_call x1, Pallas kernels: 22.1 us -> 24.8 us  [block_gradients(): pl.pallas_call(functools.partial(block_kernel, local_blocks), out_shape=(...]
where the time goes in v9:
time: 141 us
  Pallas kernels  138 us (98%)
  other arithmetic  1.75 us (1%)
    pallas_call x1, Pallas kernels, gather_rows(): pl.pallas_call(gather_kernel, out_shape=jax.ShapeDtypeStruct((RING, RING,...  62.1 us
    pallas_call x1, Pallas kernels, scatter_gradients(): pl.pallas_call(scatter_kernel, out_shape=jax.ShapeDtypeStruct((2 * edge,...  51 us
    pallas_call x1, Pallas kernels, block_gradients(): pl.pallas_call(functools.partial(block_kernel, local_blocks), out_shape=(...  24.8 us

profile of v9, /device:TPU:0, one launch (start us, length us, event | category | flops | bytes accessed | tf_op | source)
XLA Modules:
  0.0 141.1 jit_solution(6103501053045173760)
XLA Ops:
  1.3 62.1 %shard_map.94 = bf16[4,4,4,2,3,128,256]{6,5,4,3,2,1,0:T(8,128)(2,1)} custom-call(f32[3,128,256]{2,1,0:T(8,128)} %own_ref.1), custom_call_target="tpu_custom_call" | custom-call | tf_op jit(solution)/shard_map/pallas_call | solution.py:187
  63.4 0.0 copy-start
  63.4 0.0 copy-start.1
  63.4 24.8 %shard_map.95 = (f32[37,64,256]{2,1,0:T(8,128)}, s32[256]{0:T(256)}) custom-call(s32[3,36]{1,0:T(4,128)} %coords_ref.1, s32[3,256]{1,0:T(4,128)} %owner_ref.1, s32[1]{0:T(128)S(6)} %copy.10.count_ref, bf16[36,64,4096]{2,1,0:T(8,128)(2,1)} %blocks_ref.1, bf16[768,64,256]{2,1,0:T(8,128)(2,1)} %bitcast.3), custom_call_target="tpu_custom_call" | custom-call | flops 9663676416 | bytes 24772608 | tf_op jit(solution)/shard_map/pallas_call | solution.py:319
  88.2 51.0 %shard_map.96 = f32[128,256]{1,0:T(8,128)} custom-call(s32[256]{0:T(256)} %get-tuple-element.5.slot_ref, f32[37,64,256]{2,1,0:T(8,128)} %get-tuple-element.6.parts_ref), custom_call_target="tpu_custom_call" | custom-call | tf_op jit(solution)/shard_map/pallas_call | solution.py:534
  139.3 0.0 copy-done
  139.3 0.0 copy-done.1
  139.3 1.8 %bitcast_subtract_fusion = (f32[128,256]{1,0:T(8,128)}, f32[128,256]{1,0:T(8,128)}, f32[128,256]{1,0:T(8,128)}) fusion(f32[3,128,256]{2,1,0:T(8,128)} %own_ref.1, f32[128,256]{1,0:T(8,128)} %shard_map.96, f32[128,256]{1,0:T(8,128)S(1)} %copy-done, f32[128,256]{1,0:T(8,128)S(1)} %copy-done.1), kind=kLoop, calls=%fused_computation.2 | loop fusion | flops 393216 | bytes 917504 | tf_op jit(solution)/shard_map/sub | solution.py:568
Async XLA Ops:
  63.4 75.9 %copy-start = (f32[128,256]{1,0:T(8,128)S(1)}, f32[128,256]{1,0:T(8,128)}, u32[]{:S(2)}) copy-start(f32[128,256]{1,0:T(8,128)} %param.12) | copy-start | bytes 393220
  63.4 75.9 %copy-start.1 = (f32[128,256]{1,0:T(8,128)S(1)}, f32[128,256]{1,0:T(8,128)}, u32[]{:S(2)}) copy-start(f32[128,256]{1,0:T(8,128)} %param.13) | copy-start | bytes 393220

commit v10 on v9

--- a/solution.py
+++ b/solution.py
@@ -145,7 +145,6 @@
     mine.start()
     own = remote(cast_ref, table_ref.at[0, 0, 0, 1], own_sem.at[0], own_sem.at[1], place.partner())
     own.start()
-    mine.wait()
     arrive(0, 0, 0)
     arrive(0, 0, 1)
     arrive(1, 0, 0)
@@ -165,6 +164,7 @@
     begin(2, 4)
     arrive(2, 1, 1)
     arrive(2, 1, 2)
+    mine.wait()
     own.wait()
     for at in ((0, 0), (1, 0), (2, 0), (1, 1)):
         drain(*at)
@@ -278,7 +278,7 @@
     for q in range(GROUP):
         start_rows(0, 0, q)
 
-    @pl.loop(0, slot_ref.shape[0])
+    @pl.loop(0, slot_ref.shape[0], unroll=8)
     def _(p):
         slot_ref[p] = slots
 

time: 141 us -> 141 us (level)
  no operation moved by 1% of the time
where the time goes in v10:
time: 141 us
  Pallas kernels  137 us (97%)
  other arithmetic  1.75 us (1%)
    pallas_call x1, Pallas kernels, gather_rows(): pl.pallas_call(gather_kernel, out_shape=jax.ShapeDtypeStruct((RING, RING,...  62.1 us
    pallas_call x1, Pallas kernels, scatter_gradients(): pl.pallas_call(scatter_kernel, out_shape=jax.ShapeDtypeStruct((2 * edge,...  50.5 us
    pallas_call x1, Pallas kernels, block_gradients(): pl.pallas_call(functools.partial(block_kernel, local_blocks), out_shape=(...  24.9 us

profile of v10, /device:TPU:0, one launch (start us, length us, event | category | flops | bytes accessed | tf_op | source)
XLA Modules:
  0.0 140.6 jit_solution(3649585752793006527)
XLA Ops:
  1.3 62.1 %shard_map.94 = bf16[4,4,4,2,3,128,256]{6,5,4,3,2,1,0:T(8,128)(2,1)} custom-call(f32[3,128,256]{2,1,0:T(8,128)} %own_ref.1), custom_call_target="tpu_custom_call" | custom-call | tf_op jit(solution)/shard_map/pallas_call | solution.py:187
  63.4 0.0 copy-start
  63.4 0.0 copy-start.1
  63.4 24.9 %shard_map.95 = (f32[37,64,256]{2,1,0:T(8,128)}, s32[256]{0:T(256)}) custom-call(s32[3,36]{1,0:T(4,128)} %coords_ref.1, s32[3,256]{1,0:T(4,128)} %owner_ref.1, s32[1]{0:T(128)S(6)} %copy.10.count_ref, bf16[36,64,4096]{2,1,0:T(8,128)(2,1)} %blocks_ref.1, bf16[768,64,256]{2,1,0:T(8,128)(2,1)} %bitcast.3), custom_call_target="tpu_custom_call" | custom-call | flops 9663676416 | bytes 24772608 | tf_op jit(solution)/shard_map/pallas_call | solution.py:319
  88.3 50.5 %shard_map.96 = f32[128,256]{1,0:T(8,128)} custom-call(s32[256]{0:T(256)} %get-tuple-element.5.slot_ref, f32[37,64,256]{2,1,0:T(8,128)} %get-tuple-element.6.parts_ref), custom_call_target="tpu_custom_call" | custom-call | tf_op jit(solution)/shard_map/pallas_call | solution.py:534
  138.8 0.0 copy-done
  138.8 0.0 copy-done.1
  138.8 1.8 %bitcast_subtract_fusion = (f32[128,256]{1,0:T(8,128)}, f32[128,256]{1,0:T(8,128)}, f32[128,256]{1,0:T(8,128)}) fusion(f32[3,128,256]{2,1,0:T(8,128)} %own_ref.1, f32[128,256]{1,0:T(8,128)} %shard_map.96, f32[128,256]{1,0:T(8,128)S(1)} %copy-done, f32[128,256]{1,0:T(8,128)S(1)} %copy-done.1), kind=kLoop, calls=%fused_computation.2 | loop fusion | flops 393216 | bytes 917504 | tf_op jit(solution)/shard_map/sub | solution.py:568
Async XLA Ops:
  63.4 75.4 %copy-start = (f32[128,256]{1,0:T(8,128)S(1)}, f32[128,256]{1,0:T(8,128)}, u32[]{:S(2)}) copy-start(f32[128,256]{1,0:T(8,128)} %param.12) | copy-start | bytes 393220
  63.4 75.4 %copy-start.1 = (f32[128,256]{1,0:T(8,128)S(1)}, f32[128,256]{1,0:T(8,128)}, u32[]{:S(2)}) copy-start(f32[128,256]{1,0:T(8,128)} %param.13) | copy-start | bytes 393220
